TPU v7x, 512 devices: a whole 4x8x8 slice. The times are simulated.
512 devices in a mesh: seq: 32 (over x, y), grp: 16 (over z, core).
Axes of the slice: x: 4, y: 8, z: 8, core: 2. Of those that a mesh axis runs over, the one named last changes fastest.
Arguments:
- normed_hidden_input: bfloat16 [65536, 4096], P(('grp', 'seq')), may hold values from -6 to 6
- frozen_query_rows: bfloat16 [65536, 4096], P(('grp', 'seq')), may hold values from -16 to 16
- frozen_key_rows: bfloat16 [65536, 1024], P(('grp', 'seq')), may hold values from -16 to 16
- attention_output_gradient: bfloat16 [65536, 4096], P(('grp', 'seq')), may hold values from -0.15625 to 0.15625
- adapter_down_weight: bfloat16 [256, 64, 4096], P('grp', None, 'seq'), may hold values from -0.09375 to 0.09375
- adapter_up_weight: bfloat16 [256, 64, 1024], P('grp', 'seq'), may hold values from -0.75 to 0.75
- segment_adapter_index: int32 [16, 16], replicated, may hold values from 0 to 255, as said below
- segment_block_count: int32 [16, 16], replicated, may hold values from 1 to 16, 32 in all within a row
- adapter_row_index: int32 [256], replicated, may hold values from 0 to 255, as said below
Outputs:
- down_grad: float32 [256, 64, 4096], P('grp', None, 'seq')
- up_grad: float32 [256, 64, 1024], P('grp', 'seq')
Inputs may be any that keep to these rules, and one draw needn't show every extreme that they name: A permutation: adapter a is held in row adapter_row_index[a] of adapter_down_weight and adapter_up_weight. `segment_adapter_index`: call rows g * 16 to (g + 1) * 16 - 1 of adapter_down_weight the rows of index g of grp. In each sequence at most 2 segments use adapters held in the rows of one index of grp, and in every sequence some index holds exactly 2 of them. Tenants may repeat within and across sequences. `segment_block_count`: each row sums to 32; in each row some segment has exactly 16 blocks.
All inputs are finite; a program needn't handle non-finite values.
Results may differ from a plain program's by a relative error of at most 0.0056.
Values may be sent and summed in bfloat16 or wider, within the bound.
No kernel may reach another device: no remote copies, remote signals or barrier semaphores. Data moves between devices by JAX's collectives and lax.ppermute only.
A program may use at most 64 MiB of HBM per device.

v0:
```python
import math

import jax
import jax.numpy as jnp
from jax import lax
from jax.sharding import PartitionSpec as P

HEAD_DIM = 128
BLOCK = 128
QROWS = 512


adapter_scale = 2.0


def attend_head(query_head, key_head, grad_head, segment_ids, query_rows, reach):
    length, head_width = query_head.shape
    padded_keys = jnp.concatenate([jnp.zeros((reach, head_width), key_head.dtype), key_head], 0)
    padded_ids = jnp.concatenate([jnp.full((reach,), -1, jnp.int32), segment_ids], 0)
    window = query_rows + reach
    factor = 1.0 / math.sqrt(head_width)

    def one_block(totals, number):
        offset = number * query_rows
        query_block = lax.dynamic_slice_in_dim(query_head, offset, query_rows, 0)
        grad_block = lax.dynamic_slice_in_dim(grad_head, offset, query_rows, 0)
        key_block = lax.dynamic_slice_in_dim(padded_keys, offset, window, 0)
        key_ids = lax.dynamic_slice_in_dim(padded_ids, offset, window, 0)
        query_ids = lax.dynamic_slice_in_dim(segment_ids, offset, query_rows, 0)
        scores = jnp.dot(query_block, key_block.T, preferred_element_type=jnp.float32) * factor
        query_pos = offset + jnp.arange(query_rows, dtype=jnp.int32)
        key_pos = offset - reach + jnp.arange(window, dtype=jnp.int32)
        allowed = (key_ids[None, :] == query_ids[:, None]) & (
            key_pos[None, :] <= query_pos[:, None]
        )
        scores = jnp.where(allowed, scores, jnp.float32(-1e30))
        highest = jnp.max(scores, axis=1, keepdims=True)
        expo = jnp.exp(scores - highest)
        probabilities = (expo / jnp.sum(expo, axis=1, keepdims=True)).astype(jnp.bfloat16)
        contribution = jnp.dot(probabilities.T, grad_block, preferred_element_type=jnp.float32)
        current = lax.dynamic_slice_in_dim(totals, offset, window, 0)
        totals = lax.dynamic_update_slice_in_dim(totals, current + contribution, offset, 0)
        return (totals, None)

    initial = jnp.zeros((length + reach, head_width), jnp.float32)
    totals, _ = lax.scan(one_block, initial, jnp.arange(length // query_rows, dtype=jnp.int32))
    return totals[reach:].astype(jnp.bfloat16)


def local(
    normed_hidden_input,
    frozen_query_rows,
    frozen_key_rows,
    attention_output_gradient,
    adapter_down_weight,
    adapter_up_weight,
    segment_adapter_index,
    segment_block_count,
    adapter_row_index,
):
    group_count = lax.axis_size("grp")
    shard_count = lax.axis_size("seq")
    group_index = lax.axis_index("grp")
    tokens_here, model_width = normed_hidden_input.shape
    portion_width = adapter_down_weight.shape[2]
    resident_adapters, rank_overall = (adapter_down_weight.shape[0], adapter_down_weight.shape[1])
    rank_portion, value_projection_width = (adapter_up_weight.shape[1], adapter_up_weight.shape[2])
    segments = segment_adapter_index.shape[1]
    capacity = max(2, (segments + group_count - 1) // group_count)
    seq_length = tokens_here * shard_count
    block_total = seq_length // BLOCK
    block_here = tokens_here // BLOCK
    reach = min(16, seq_length // (2 * BLOCK)) * BLOCK
    head_total = frozen_query_rows.shape[1] // HEAD_DIM
    kv_heads = value_projection_width // HEAD_DIM
    heads_here = head_total // shard_count
    group_size = head_total // kv_heads
    slot_total = group_count * capacity
    adapter_ids = jnp.arange(adapter_row_index.shape[0], dtype=jnp.int32)
    slot_of = jnp.sum(
        jnp.where(segment_adapter_index[:, :, None] == adapter_ids, adapter_row_index, 0), axis=2
    )
    owner_group = slot_of // resident_adapters
    local_slot = slot_of % resident_adapters
    order_ids = jnp.arange(segments, dtype=jnp.int32)
    earlier = order_ids[:, None] > order_ids[None, :]
    same_owner = owner_group[:, :, None] == owner_group[:, None, :]
    rank_in_owner = jnp.sum((same_owner & earlier[None]).astype(jnp.int32), axis=2)
    placement = owner_group * capacity + rank_in_owner
    capacity_ids = jnp.arange(capacity, dtype=jnp.int32)
    local_ids = jnp.arange(resident_adapters, dtype=jnp.int32)
    picks = (
        (owner_group == group_index)[:, :, None, None]
        & (rank_in_owner[:, :, None, None] == capacity_ids[:, None])
        & (local_slot[:, :, None, None] == local_ids)
    )
    chooser = jnp.sum(picks.astype(jnp.float32), axis=1)
    selector_half = chooser.astype(jnp.bfloat16)
    send_down = jnp.einsum(
        "pgl,lut->pgut", selector_half, adapter_down_weight, preferred_element_type=jnp.float32
    ).astype(jnp.bfloat16)
    send_up = jnp.einsum(
        "gyv,vmf->gymf", selector_half, adapter_up_weight, preferred_element_type=jnp.float32
    ).astype(jnp.bfloat16)
    fetched_down, fetched_up = (
        lax.all_to_all(send_down, "grp", split_axis=0, concat_axis=0, tiled=True),
        lax.all_to_all(send_up, "grp", split_axis=0, concat_axis=0, tiled=True),
    )
    own_blocks = segment_block_count[group_index]
    ends = jnp.cumsum(own_blocks)
    block_seg = jnp.sum(
        (jnp.arange(block_total, dtype=jnp.int32)[:, None] >= ends[None, :]).astype(jnp.int32),
        axis=1,
    )
    own_place = placement[group_index]
    block_place = jnp.sum(
        jnp.where(block_seg[:, None] == order_ids[None, :], own_place[None, :], 0), axis=1
    )
    block_pick = block_place[:, None] == jnp.arange(slot_total, dtype=jnp.int32)[None, :]
    pick_half = block_pick.astype(jnp.bfloat16)
    segment_ids = jnp.broadcast_to(block_seg[:, None], (block_total, BLOCK)).reshape(seq_length)
    block_down_weight = jnp.einsum(
        "bn,nrd->brd",
        pick_half,
        fetched_down.reshape(slot_total, rank_overall, portion_width),
        preferred_element_type=jnp.float32,
    ).astype(jnp.bfloat16)
    block_up_rows = jnp.einsum(
        "bn,nre->bre",
        pick_half,
        fetched_up.reshape(slot_total, rank_portion, value_projection_width),
        preferred_element_type=jnp.float32,
    ).astype(jnp.bfloat16)
    features = lax.all_to_all(normed_hidden_input, "seq", split_axis=1, concat_axis=0, tiled=True)
    amount = lax.axis_size("seq") * tokens_here
    token_rows = features.reshape(amount // BLOCK, BLOCK, portion_width)
    reduced_rank_part = (
        lax.psum_scatter(
            jnp.einsum(
                "jyw,jaw->jya", token_rows, block_down_weight, preferred_element_type=jnp.float32
            ).reshape(amount, rank_overall),
            "seq",
            scatter_dimension=0,
            tiled=True,
        )
        .astype(jnp.bfloat16)
        .reshape(block_here, BLOCK, rank_overall)
    )
    near_up = lax.all_to_all(block_up_rows, "seq", split_axis=0, concat_axis=1, tiled=True)
    query_grid = frozen_query_rows.reshape(tokens_here, shard_count, heads_here, HEAD_DIM)
    key_grid = jnp.repeat(
        frozen_key_rows.reshape(tokens_here, kv_heads, HEAD_DIM), group_size, axis=1
    ).reshape(tokens_here, shard_count, heads_here, HEAD_DIM)
    grad_grid = attention_output_gradient.reshape(tokens_here, shard_count, heads_here, HEAD_DIM)
    query_all = lax.all_to_all(query_grid, "seq", split_axis=1, concat_axis=0, tiled=True)
    key_all = lax.all_to_all(key_grid, "seq", split_axis=1, concat_axis=0, tiled=True)
    grad_all = lax.all_to_all(grad_grid, "seq", split_axis=1, concat_axis=0, tiled=True)

    def per_head(triple):
        return attend_head(triple[0], triple[1], triple[2], segment_ids, QROWS, reach)

    stacked = (
        jnp.moveaxis(query_all[:, 0], 1, 0),
        jnp.moveaxis(key_all[:, 0], 1, 0),
        jnp.moveaxis(grad_all[:, 0], 1, 0),
    )
    result = lax.map(per_head, stacked)
    head_grads = jnp.moveaxis(result, 0, 1)[:, None]
    token_grads = lax.all_to_all(head_grads, "seq", split_axis=0, concat_axis=1, tiled=True)
    value_grad = jnp.sum(
        token_grads.reshape(tokens_here, kv_heads, group_size, HEAD_DIM), axis=2, dtype=jnp.float32
    )
    value_row_blocks = value_grad.reshape(block_here, BLOCK, value_projection_width).astype(
        jnp.bfloat16
    )
    up_weight_terms = adapter_scale * jnp.einsum(
        "fvg,fvn->fgn", reduced_rank_part, value_row_blocks, preferred_element_type=jnp.float32
    )
    backward_rank_part = (
        adapter_scale
        * jnp.einsum("vaw,vpw->vap", value_row_blocks, near_up, preferred_element_type=jnp.float32)
    ).astype(jnp.bfloat16)
    all_low = lax.all_gather(
        backward_rank_part.reshape(tokens_here, rank_overall), "seq", axis=0, tiled=True
    )
    back_down = jnp.einsum(
        "jcy,jct->jyt",
        all_low.reshape(block_total, BLOCK, rank_overall),
        features.reshape(block_total, BLOCK, portion_width),
        preferred_element_type=jnp.float32,
    )
    back_up = lax.all_to_all(up_weight_terms, "seq", split_axis=1, concat_axis=0, tiled=True)
    pick_full = block_pick.astype(jnp.float32)
    slot_down = jnp.einsum("bn,brd->nrd", pick_full, back_down, precision=lax.Precision.HIGHEST)
    slot_up = jnp.einsum("bn,bre->nre", pick_full, back_up, precision=lax.Precision.HIGHEST)
    return_down, return_up = (
        lax.all_to_all(
            slot_down.reshape(group_count, capacity, rank_overall, portion_width),
            "grp",
            split_axis=0,
            concat_axis=0,
            tiled=True,
        ),
        lax.all_to_all(
            slot_up.reshape(group_count, capacity, rank_portion, value_projection_width),
            "grp",
            split_axis=0,
            concat_axis=0,
            tiled=True,
        ),
    )
    down_grad = jnp.einsum("nca,ncrd->ard", chooser, return_down, precision=lax.Precision.HIGHEST)
    up_grad = jnp.einsum("nca,ncre->are", chooser, return_up, precision=lax.Precision.HIGHEST)
    return (down_grad, up_grad)


def solution(mesh):
    return jax.shard_map(
        local,
        mesh=mesh,
        in_specs=(
            P(("grp", "seq"), None),
            P(("grp", "seq"), None),
            P(("grp", "seq"), None),
            P(("grp", "seq"), None),
            P("grp", None, "seq"),
            P("grp", "seq", None),
            P(),
            P(),
            P(),
        ),
        out_specs=(P("grp", None, "seq"), P("grp", "seq", None)),
        check_vma=False,
    )
```

profile of v0, /device:TPU:1, one launch (start us, length us, event | category | flops | bytes accessed | tf_op | source)
XLA Modules:
  0.0 591.7 jit_solution(1120349917430718640)
XLA Ops:
  11.0 11.8 %all-to-all-start.4 = ((bf16[16,2,2,1024]{3,2,1,0:T(2,128)(2,1)}), bf16[16,2,2,1024]{3,2,1,0:T(2,128)(2,1)S(1)}, u32[]{:S(2)}, u32[]{:S(2)}) async-start(bf16[16,2,2,1024]{3,2,1,0:T(2,128)(2,1)} %copy.109), calls=%async_computation.4 | async-start | bytes 262144 | tf_op jit(solution)/shard_map/all_to_all | solution.py:107
  25.0 7.0 %all-to-all-done.4 = bf16[16,2,2,1024]{3,2,1,0:T(2,128)(2,1)S(1)} async-done(((bf16[16,2,2,1024]{3,2,1,0:T(2,128)(2,1)}), bf16[16,2,2,1024]{3,2,1,0:T(2,128)(2,1)S(1)}, u32[]{:S(2)}, u32[]{:S(2)}) %all-to-all-start.4) | async-done | bytes 131104 | tf_op jit(solution)/shard_map/all_to_all | solution.py:107
  35.5 16.8 %all-to-all-done.8 = bf16[16,2,64,128]{3,2,1,0:T(8,128)(2,1)S(1)} async-done(((bf16[16,2,64,128]{3,2,1,0:T(8,128)(2,1)}), bf16[16,2,64,128]{3,2,1,0:T(8,128)(2,1)S(1)}, u32[]{:S(2)}, u32[]{:S(2)}) %all-to-all-start.8) | async-done | bytes 524320 | tf_op jit(solution)/shard_map/all_to_all | solution.py:106
  53.5 9.7 %all-to-all-start.1 = ((bf16[128,32,1,128]{3,0,2,1:T(8,128)(2,1)}), bf16[128,32,1,128]{3,0,2,1:T(8,128)(2,1)S(1)}, u32[]{:S(2)}, u32[]{:S(2)}) async-start(bf16[128,32,1,128]{3,0,2,1:T(8,128)(2,1)} %bitcast.10), calls=%async_computation.1 | async-start | bytes 2097152 | tf_op jit(solution)/shard_map/all_to_all | solution.py:156
  66.2 25.2 %all-to-all-done.1 = bf16[128,32,1,128]{3,0,2,1:T(8,128)(2,1)S(1)} async-done(((bf16[128,32,1,128]{3,0,2,1:T(8,128)(2,1)}), bf16[128,32,1,128]{3,0,2,1:T(8,128)(2,1)S(1)}, u32[]{:S(2)}, u32[]{:S(2)}) %all-to-all-start.1) | async-done | bytes 1048608 | tf_op jit(solution)/shard_map/all_to_all | solution.py:156
  91.4 5.6 all-to-all-start.2
  99.9 22.2 %all-to-all-done.2 = bf16[128,32,1,128]{3,0,2,1:T(8,128)(2,1)} async-done(((bf16[128,32,1,128]{3,0,2,1:T(8,128)(2,1)}), bf16[128,32,1,128]{3,0,2,1:T(8,128)(2,1)}, u32[]{:S(2)}, u32[]{:S(2)}) %all-to-all-start.2) | async-done | bytes 1048608 | tf_op jit(solution)/shard_map/all_to_all | solution.py:157
  122.2 8.1 %all-to-all-start = ((bf16[128,32,1,128]{3,0,2,1:T(8,128)(2,1)}), bf16[128,32,1,128]{3,0,2,1:T(8,128)(2,1)}, u32[]{:S(2)}, u32[]{:S(2)}) async-start(bf16[128,32,1,128]{3,0,2,1:T(8,128)(2,1)} %copy.101), calls=%async_computation | async-start | bytes 2097152 | tf_op jit(solution)/shard_map/all_to_all | solution.py:155
  135.8 19.1 %all-to-all-done = bf16[128,32,1,128]{3,0,2,1:T(8,128)(2,1)} async-done(((bf16[128,32,1,128]{3,0,2,1:T(8,128)(2,1)}), bf16[128,32,1,128]{3,0,2,1:T(8,128)(2,1)}, u32[]{:S(2)}, u32[]{:S(2)}) %all-to-all-start) | async-done | bytes 1048608 | tf_op jit(solution)/shard_map/all_to_all | solution.py:155
  154.9 8.6 %all-to-all-start.6 = ((bf16[128,32,128]{2,0,1:T(8,128)(2,1)}), bf16[128,32,128]{2,0,1:T(8,128)(2,1)S(1)}, u32[]{:S(2)}, u32[]{:S(2)}) async-start(bf16[128,32,128]{2,0,1:T(8,128)(2,1)} %copy.113), calls=%async_computation.6 | async-start | bytes 2097152 | tf_op jit(solution)/shard_map/all_to_all | solution.py:134
  165.3 67.9 %while.19 = (s32[]{:T(128)}, f32[6144,128]{1,0:T(8,128)}, s32[8]{0:T(128)S(1)}, s32[6144]{0:T(1024)S(1)}, s32[4096]{0:T(1024)S(1)}, /*index=5*/bf16[4096,128]{1,...) while((s32[]{:T(128)}, f32[6144,128]{1,0:T(8,128)}, ...), condition=%wide.region_9.10_spmd, body=%wide.region_6.9_spmd.sunk | while | flops 685836288 | bytes 19343620 | solution.py:46
  187.0 3.8 fusion.64
  195.5 3.8 fusion.64
  204.0 3.8 fusion.64
  238.1 9.2 %all-to-all-start.3 = ((bf16[32,2,8192]{2,1,0:T(2,128)(2,1)}), bf16[32,2,8192]{2,1,0:T(2,128)(2,1)S(1)}, u32[]{:S(2)}, u32[]{:S(2)}) async-start(bf16[32,2,8192]{2,1,0:T(2,128)(2,1)} %reshape.260), calls=%async_computation.3 | async-start | bytes 2097152 | tf_op jit(solution)/shard_map/all_to_all | solution.py:169
  251.6 20.3 %all-to-all-done.3 = bf16[32,2,8192]{2,1,0:T(2,128)(2,1)S(1)} async-done(((bf16[32,2,8192]{2,1,0:T(2,128)(2,1)}), bf16[32,2,8192]{2,1,0:T(2,128)(2,1)S(1)}, u32[]{:S(2)}, u32[]{:S(2)}) %all-to-all-start.3) | async-done | bytes 1048608 | tf_op jit(solution)/shard_map/all_to_all | solution.py:169
  272.9 8.3 %all-to-all-start.5 = ((bf16[32,2,1024]{2,1,0:T(2,128)(2,1)}), bf16[32,2,1024]{2,1,0:T(2,128)(2,1)S(1)}, u32[]{:S(2)}, u32[]{:S(2)}) async-start(bf16[32,2,1024]{2,1,0:T(2,128)(2,1)} %copy.111), calls=%async_computation.5 | async-start | bytes 262144 | tf_op jit(solution)/shard_map/all_to_all | solution.py:149
  281.3 4.3 reshape.261
  288.3 176.5 %reduce-scatter.2.cloned.1.call-done = f32[128,64]{0,1:T(8,128)} async-done(((f32[4096,64]{0,1:T(8,128)}), f32[128,64]{0,1:T(8,128)}) %reduce-scatter.2.cloned.1.call-update) | async-done | bytes 32784 | tf_op jit(solution)/shard_map/reduce_scatter | solution.py:138
  466.8 6.5 %all-to-all-start.9 = ((f32[1,64,1024]{2,0,1:T(1,128)}), f32[1,64,1024]{2,0,1:T(1,128)S(1)}, u32[]{:S(2)}, u32[]{:S(2)}) async-start(f32[1,64,1024]{2,0,1:T(1,128)} %copy.126), calls=%async_computation.10 | async-start | bytes 524288 | tf_op jit(solution)/shard_map/all_to_all | solution.py:192
  473.5 39.6 %all_gather.3 = bf16[4096,64]{0,1:T(8,128)(2,1)S(1)} all-gather(bf16[128,64]{0,1:T(8,128)(2,1)S(1)} %fusion.8), channel_id=1, replica_groups=mesh['seq'=32,'grp'=16] {'seq'}, dimensions={0}, use_global_device_ids=true | all-gather | bytes 540672 | tf_op jit(solution)/shard_map/all_gather | solution.py:183
  515.2 25.0 %all-to-all-start.10 = ((f32[16,2,2,1024]{3,1,2,0:T(2,128)}), f32[16,2,2,1024]{3,1,2,0:T(2,128)S(1)}, u32[]{:S(2)}, u32[]{:S(2)}) async-start(f32[16,2,2,1024]{3,1,2,0:T(2,128)} %copy.128), calls=%async_computation.11 | async-start | bytes 524288 | tf_op jit(solution)/shard_map/all_to_all | solution.py:204
  543.5 8.4 %all-to-all-done.10 = f32[16,2,2,1024]{3,1,2,0:T(2,128)S(1)} async-done(((f32[16,2,2,1024]{3,1,2,0:T(2,128)}), f32[16,2,2,1024]{3,1,2,0:T(2,128)S(1)}, u32[]{:S(2)}, u32[]{:S(2)}) %all-to-all-start.10) | async-done | bytes 262176 | tf_op jit(solution)/shard_map/all_to_all | solution.py:204
  556.7 26.0 %all-to-all-done.7 = f32[16,2,64,128]{3,1,2,0:T(2,128)S(1)} async-done(((f32[16,2,64,128]{3,1,2,0:T(2,128)}), f32[16,2,64,128]{3,1,2,0:T(2,128)S(1)}, u32[]{:S(2)}, u32[]{:S(2)}) %all-to-all-start.7) | async-done | bytes 1048608 | tf_op jit(solution)/shard_map/all_to_all | solution.py:197
  (139 shorter events, 102.4 us)
Async XLA Ops:
  7.2 28.3 %copy-start = (bf16[128,1024]{1,0:T(8,128)(2,1)S(1)}, bf16[128,1024]{1,0:T(8,128)(2,1)}, u32[]{:S(2)}) copy-start(bf16[128,1024]{1,0:T(8,128)(2,1)} %param.13) | copy-start | bytes 786436
  11.0 21.0 %all-to-all-start.4 = ((bf16[16,2,2,1024]{3,2,1,0:T(2,128)(2,1)}), bf16[16,2,2,1024]{3,2,1,0:T(2,128)(2,1)S(1)}, u32[]{:S(2)}, u32[]{:S(2)}) async-start(bf16[16,2,2,1024]{3,2,1,0:T(2,128)(2,1)} %copy.109), calls=%async_computation.4 | async-start | bytes 262144 | tf_op jit(solution)/shard_map/all_to_all | solution.py:107
  32.0 20.3 %all-to-all-start.8 = ((bf16[16,2,64,128]{3,2,1,0:T(8,128)(2,1)}), bf16[16,2,64,128]{3,2,1,0:T(8,128)(2,1)S(1)}, u32[]{:S(2)}, u32[]{:S(2)}) async-start(bf16[16,2,64,128]{3,2,1,0:T(8,128)(2,1)} %copy.122), calls=%async_computation.8 | async-start | bytes 1048576 | tf_op jit(solution)/shard_map/all_to_all | solution.py:106
  53.5 37.9 %all-to-all-start.1 = ((bf16[128,32,1,128]{3,0,2,1:T(8,128)(2,1)}), bf16[128,32,1,128]{3,0,2,1:T(8,128)(2,1)S(1)}, u32[]{:S(2)}, u32[]{:S(2)}) async-start(bf16[128,32,1,128]{3,0,2,1:T(8,128)(2,1)} %bitcast.10), calls=%async_computation.1 | async-start | bytes 2097152 | tf_op jit(solution)/shard_map/all_to_all | solution.py:156
  91.4 30.8 %all-to-all-start.2 = ((bf16[128,32,1,128]{3,0,2,1:T(8,128)(2,1)}), bf16[128,32,1,128]{3,0,2,1:T(8,128)(2,1)}, u32[]{:S(2)}, u32[]{:S(2)}) async-start(bf16[128,32,1,128]{3,0,2,1:T(8,128)(2,1)} %copy.104), calls=%async_computation.2 | async-start | bytes 2097152 | tf_op jit(solution)/shard_map/all_to_all | solution.py:157
  122.2 32.7 %all-to-all-start = ((bf16[128,32,1,128]{3,0,2,1:T(8,128)(2,1)}), bf16[128,32,1,128]{3,0,2,1:T(8,128)(2,1)}, u32[]{:S(2)}, u32[]{:S(2)}) async-start(bf16[128,32,1,128]{3,0,2,1:T(8,128)(2,1)} %copy.101), calls=%async_computation | async-start | bytes 2097152 | tf_op jit(solution)/shard_map/all_to_all | solution.py:155
  134.4 30.9 %copy-start.2 = (s32[32]{0:T(128)}, s32[32]{0:T(128)S(1)}, u32[]{:S(2)}) copy-start(s32[32]{0:T(128)S(1)} %select_reduce_fusion.1) | copy-start | bytes 388
  154.9 83.2 %all-to-all-start.6 = ((bf16[128,32,128]{2,0,1:T(8,128)(2,1)}), bf16[128,32,128]{2,0,1:T(8,128)(2,1)S(1)}, u32[]{:S(2)}, u32[]{:S(2)}) async-start(bf16[128,32,128]{2,0,1:T(8,128)(2,1)} %copy.113), calls=%async_computation.6 | async-start | bytes 2097152 | tf_op jit(solution)/shard_map/all_to_all | solution.py:134
  238.1 12.4 %copy-start.3 = (s32[32]{0:T(128)S(1)}, s32[32]{0:T(128)}, u32[]{:S(2)}) copy-start(s32[32]{0:T(128)} %copy-done.2) | copy-start | bytes 388
  238.1 33.8 %all-to-all-start.3 = ((bf16[32,2,8192]{2,1,0:T(2,128)(2,1)}), bf16[32,2,8192]{2,1,0:T(2,128)(2,1)S(1)}, u32[]{:S(2)}, u32[]{:S(2)}) async-start(bf16[32,2,8192]{2,1,0:T(2,128)(2,1)} %reshape.260), calls=%async_computation.3 | async-start | bytes 2097152 | tf_op jit(solution)/shard_map/all_to_all | solution.py:169
  247.4 217.5 %reduce-scatter.2.cloned.1.call-start = ((), (), s32[]{:S(2)}) async-start(), calls=%async_computation.12 | async-start | bytes 1081344 | tf_op jit(solution)/shard_map/reduce_scatter | solution.py:138
  271.9 1.0 copy-start.1
  272.9 193.9 %all-to-all-start.5 = ((bf16[32,2,1024]{2,1,0:T(2,128)(2,1)}), bf16[32,2,1024]{2,1,0:T(2,128)(2,1)S(1)}, u32[]{:S(2)}, u32[]{:S(2)}) async-start(bf16[32,2,1024]{2,1,0:T(2,128)(2,1)} %copy.111), calls=%async_computation.5 | async-start | bytes 262144 | tf_op jit(solution)/shard_map/all_to_all | solution.py:149
  286.7 227.2 %copy-start.4 = (s32[32]{0:T(128)S(1)}, s32[32]{0:T(128)}, u32[]{:S(2)}) copy-start(s32[32]{0:T(128)} %copy-done.2) | copy-start | bytes 388
  466.8 46.3 %all-to-all-start.9 = ((f32[1,64,1024]{2,0,1:T(1,128)}), f32[1,64,1024]{2,0,1:T(1,128)S(1)}, u32[]{:S(2)}, u32[]{:S(2)}) async-start(f32[1,64,1024]{2,0,1:T(1,128)} %copy.126), calls=%async_computation.10 | async-start | bytes 524288 | tf_op jit(solution)/shard_map/all_to_all | solution.py:192
  515.2 36.7 %all-to-all-start.10 = ((f32[16,2,2,1024]{3,1,2,0:T(2,128)}), f32[16,2,2,1024]{3,1,2,0:T(2,128)S(1)}, u32[]{:S(2)}, u32[]{:S(2)}) async-start(f32[16,2,2,1024]{3,1,2,0:T(2,128)} %copy.128), calls=%async_computation.11 | async-start | bytes 524288 | tf_op jit(solution)/shard_map/all_to_all | solution.py:204
  551.9 30.8 %all-to-all-start.7 = ((f32[16,2,64,128]{3,1,2,0:T(2,128)}), f32[16,2,64,128]{3,1,2,0:T(2,128)S(1)}, u32[]{:S(2)}, u32[]{:S(2)}) async-start(f32[16,2,64,128]{3,1,2,0:T(2,128)} %copy.117), calls=%async_computation.7 | async-start | bytes 2097152 | tf_op jit(solution)/shard_map/all_to_all | solution.py:197
Sparse Core Ops, SparseCore 0:
  252.6 212.2 reduce-scatter.1
where the time goes:
time: 594 us; the launch traced here: 592 us
  waiting for transfers between devices  322 us (54%)
  starting transfers between devices  100 us (17%)
  matrix products  60.2 us (10%)
  blocking collectives  39.6 us (7%)
  local copies, waits for them, and re-layouts  38.2 us (6%)
  between operations  14.4 us (2%)
  other arithmetic  12.6 us (2%)
    reduce_scatter x1, waiting for transfers between devices, local(): lax.psum_scatter(jnp.einsum('jyw,jaw->jya', token_rows, block_down_weight...  177 us
    all_gather x1, blocking collectives, local(): lax.all_gather(backward_rank_part.reshape(tokens_here, rank_overall), 'se...  39.6 us
    dot_general x8, matrix products, one_block(): jnp.dot(probabilities.T, grad_block, preferred_element_type=jnp.float32)  30.3 us
    all_to_all x1, waiting for transfers between devices, local(): lax.all_to_all(slot_down.reshape(group_count, capacity, rank_overall, por...  26 us
    all_to_all x1, waiting for transfers between devices, local(): lax.all_to_all(key_grid, 'seq', split_axis=1, concat_axis=0, tiled=True)  25.2 us
    all_to_all x1, starting transfers between devices, local(): lax.all_to_all(slot_up.reshape(group_count, capacity, rank_portion, value...  25 us
    all_to_all x1, waiting for transfers between devices, local(): lax.all_to_all(grad_grid, 'seq', split_axis=1, concat_axis=0, tiled=True)  22.2 us
    all_to_all x1, waiting for transfers between devices, local(): lax.all_to_all(head_grads, 'seq', split_axis=0, concat_axis=1, tiled=True)  20.3 us
  transfers between devices with their start and end apart: 12, of which 9 were waited for; matrix products, arithmetic and copies ran while one was open for 17% of the time, Pallas kernels for 0%

commit v1 on v0

v1 whole, which is shorter than its diff:
```python
import functools
import math

import jax
import jax.numpy as jnp
from jax import lax
from jax.experimental import pallas as pl
from jax.experimental.pallas import tpu as pltpu
from jax.sharding import PartitionSpec as P

HEAD_DIM = 128
BLOCK = 128
LONG = 16
CAP = 2
ROWS = 80
NEG = -1e30
FACTOR = 1.0 / math.sqrt(HEAD_DIM)

COLUMN = [[8 * x + 2 * q + p for x in range(4) for p in range(2)] for q in range(4)]
ROW = [[8 * x + 2 * q + p for q in range(4)] for x in range(4) for p in range(2)]

VMEM = pl.BlockSpec(memory_space=pltpu.VMEM)
ANY = pl.BlockSpec(memory_space=pl.ANY)
F32 = jnp.float32
BF16 = jnp.bfloat16


def dot_nt(a, b):
    return lax.dot_general(a, b, (((1,), (1,)), ((), ())), preferred_element_type=F32)


def dot_tn(a, b):
    return lax.dot_general(a, b, (((0,), (0,)), ((), ())), preferred_element_type=F32)


def dot_nn(a, b):
    return jnp.dot(a, b, preferred_element_type=F32)


def stack_heads(rows):
    return jnp.concatenate([rows[:, h * 128 : (h + 1) * 128] for h in range(4)], axis=0)


def pack_kernel(q_ref, g_ref, k_ref, out_ref):
    for h in range(8):
        out_ref[h, :, :512] = q_ref[:, 512 * h : 512 * (h + 1)]
        out_ref[h, :, 512:1024] = g_ref[:, 512 * h : 512 * (h + 1)]
        out_ref[h, :, 1024:] = k_ref[:, 128 * h : 128 * (h + 1)]


def pack(q, g, k):
    return pl.pallas_call(
        pack_kernel,
        name="pack",
        out_shape=jax.ShapeDtypeStruct((8, 128, 1152), BF16),
        grid=(4,),
        in_specs=[
            pl.BlockSpec((32, 4096), lambda i: (i, 0)),
            pl.BlockSpec((32, 4096), lambda i: (i, 0)),
            pl.BlockSpec((32, 1024), lambda i: (i, 0)),
        ],
        out_specs=pl.BlockSpec((8, 32, 1152), lambda i: (0, i, 0)),
        cost_estimate=pl.CostEstimate(flops=0, bytes_accessed=5 << 20, transcendentals=0),
    )(q, g, k)


def pick_kernel(slot_ref, all_ref, out_ref, sems):
    started = [
        pltpu.make_async_copy(all_ref.at[slot_ref[b]], out_ref.at[b], sems.at[b]) for b in range(32)
    ]
    for c in started:
        c.start()
    for c in started:
        c.wait()


def pick(slots, gathered):
    return pl.pallas_call(
        pick_kernel,
        name="pick",
        out_shape=jax.ShapeDtypeStruct((32, ROWS, 128), BF16),
        in_specs=[pl.BlockSpec(memory_space=pltpu.SMEM), ANY],
        out_specs=VMEM,
        scratch_shapes=[pltpu.SemaphoreType.DMA((32,))],
        cost_estimate=pl.CostEstimate(flops=0, bytes_accessed=1 << 20, transcendentals=0),
    )(slots, gathered)


def long_kernel(tab_ref, recv_ref, key_ref, out_ref, keys, acc, sc):
    i = pl.program_id(0)

    @pl.when(i == 0)
    def _():
        acc[...] = jnp.zeros_like(acc)
        for j in range(LONG):
            keys[pl.ds(128 * j, 128), :] = key_ref[tab_ref[8 + j]]

    own = recv_ref[0]
    queries = stack_heads(own[:, :512])
    grads = stack_heads(own[:, 512:1024])
    pos = tab_ref[4 + i]
    last = pos // 2

    def scores(c):
        start = pl.multiple_of(c * 256, 256)
        return dot_nt(keys[pl.ds(start, 256), :], queries) * FACTOR

    def fold(s):
        return jnp.max(s.reshape(32, 8, 512), axis=0)

    def first(c, top):
        s = scores(c)
        sc[c] = s
        return jnp.maximum(top, fold(s))

    s = scores(last)
    key_at = lax.broadcasted_iota(jnp.int32, (256, 512), 0) + last * 256
    query_at = (lax.broadcasted_iota(jnp.int32, (256, 512), 1) & 127) + pos * 128
    s = jnp.where(key_at <= query_at, s, NEG)
    sc[last] = s
    top = lax.fori_loop(0, last, first, fold(s))
    top = jnp.max(top, axis=0, keepdims=True)

    def second(c, total):
        e = jnp.exp(sc[c] - top)
        sc[c] = e
        return total + jnp.sum(e.reshape(32, 8, 512), axis=0)

    total = lax.fori_loop(0, last + 1, second, jnp.zeros((8, 512), F32))
    inverse = 1.0 / jnp.sum(total, axis=0, keepdims=True)

    def third(c, carry):
        p = (sc[c] * inverse).astype(BF16)
        rows = pl.ds(pl.multiple_of(c * 256, 256), 256)
        acc[rows, :] += dot_nn(p, grads)
        return carry

    lax.fori_loop(0, last + 1, third, 0)

    @pl.when(i == 3)
    def _():
        for j in range(LONG):
            out_ref[tab_ref[24 + j]] = acc[pl.ds(128 * j, 128), :].astype(BF16)


def long_attention(table, recv, keys):
    return pl.pallas_call(
        long_kernel,
        name="long",
        out_shape=jax.ShapeDtypeStruct((LONG, 128, 128), BF16),
        grid_spec=pltpu.PrefetchScalarGridSpec(
            num_scalar_prefetch=1,
            grid=(4,),
            in_specs=[
                pl.BlockSpec((1, 128, 1152), lambda i, t: (t[i], 0, 0)),
                pl.BlockSpec((LONG, 128, 128), lambda i, t: (0, 0, 0)),
            ],
            out_specs=pl.BlockSpec((LONG, 128, 128), lambda i, t: (0, 0, 0)),
            scratch_shapes=[
                pltpu.VMEM((2048, 128), BF16),
                pltpu.VMEM((2048, 128), F32),
                pltpu.VMEM((8, 256, 512), F32),
            ],
        ),
        compiler_params=pltpu.CompilerParams(vmem_limit_bytes=32 << 20),
        cost_estimate=pl.CostEstimate(
            flops=6 << 30, bytes_accessed=3 << 20, transcendentals=8 << 20
        ),
    )(table, recv, keys)


def short_kernel(tab_ref, q_ref, g_ref, k_ref, left_ref, own_ref, prev_ref):
    queries = stack_heads(q_ref[...])
    key_at = lax.broadcasted_iota(jnp.int32, (128, 512), 0)
    query_at = lax.broadcasted_iota(jnp.int32, (128, 512), 1) & 127
    own = jnp.where(key_at <= query_at, dot_nt(k_ref[...], queries) * FACTOR, NEG)
    joined = tab_ref[0] > 0
    prev = jnp.where(joined, dot_nt(left_ref[...], queries) * FACTOR, NEG)
    top = jnp.maximum(jnp.max(own, axis=0, keepdims=True), jnp.max(prev, axis=0, keepdims=True))
    own = jnp.exp(own - top)
    prev = jnp.exp(prev - top)
    total = jnp.sum(own, axis=0, keepdims=True) + jnp.sum(prev, axis=0, keepdims=True)
    inverse = 1.0 / total
    own = (own * inverse).astype(BF16)
    prev = (prev * inverse).astype(BF16)
    summed = jnp.zeros((128, 128), F32)
    for h in range(4):
        lanes = slice(h * 128, (h + 1) * 128)
        summed += dot_nn(own[:, lanes], g_ref[:, lanes]).astype(BF16).astype(F32)
    own_ref[...] = summed
    prev_ref[...] = dot_nn(prev, stack_heads(g_ref[...])).astype(BF16)


def short_attention(table, q, g, k, left):
    wide = pl.BlockSpec((128, 512), lambda i, t: (0, i))
    thin = pl.BlockSpec((128, 128), lambda i, t: (0, i))
    return pl.pallas_call(
        short_kernel,
        name="short",
        out_shape=(
            jax.ShapeDtypeStruct((128, 1024), F32),
            jax.ShapeDtypeStruct((128, 1024), BF16),
        ),
        grid_spec=pltpu.PrefetchScalarGridSpec(
            num_scalar_prefetch=1,
            grid=(8,),
            in_specs=[wide, wide, thin, thin],
            out_specs=(thin, thin),
        ),
        cost_estimate=pl.CostEstimate(
            flops=3 << 30, bytes_accessed=4 << 20, transcendentals=4 << 20
        ),
    )(table, q, g, k, left)


def interleave(transposed):
    row = lax.broadcasted_iota(jnp.int32, (512, 512), 0)
    col = lax.broadcasted_iota(jnp.int32, (512, 512), 1)
    if transposed:
        row, col = col, row
    return (col == (row & 7) * 64 + (row >> 3)).astype(BF16)


def terms_kernel(tab_ref, x_ref, w_ref, far_ref, own_ref, right_ref, out_ref, down):
    for s in range(32):
        down[:, 128 * s : 128 * (s + 1)] = w_ref[s, :64, :]
    low = dot_nt(x_ref[...], down[...]).astype(BF16)
    up = dot_nn(interleave(True), w_ref[:, 64:, :].reshape(512, 128)).astype(BF16)
    is_long = tab_ref[2] > 0
    is_first = tab_ref[1] > 0
    back = jnp.zeros((128, 64), F32)
    up_terms = []
    for c in range(8):
        lanes = slice(c * 128, (c + 1) * 128)
        near = own_ref[:, lanes] + jnp.where(is_first, right_ref[:, lanes].astype(F32), 0.0)
        value = jnp.where(is_long, far_ref[c].astype(F32), near).astype(BF16)
        back += dot_nt(value, up[64 * c : 64 * (c + 1), :])
        up_terms.append((2.0 * dot_tn(low, value)).astype(BF16))
    mixed = dot_nn(interleave(False), jnp.concatenate(up_terms, axis=0)).astype(BF16)
    out_ref[:, 64:, :] = mixed.reshape(32, 16, 128)
    back = (2.0 * back).astype(BF16)
    for s in range(32):
        out_ref[s, :64, :] = dot_tn(back, x_ref[:, 128 * s : 128 * (s + 1)]).astype(BF16)


def terms(table, x, weights, far, own, right):
    return pl.pallas_call(
        terms_kernel,
        name="terms",
        out_shape=jax.ShapeDtypeStruct((32, ROWS, 128), BF16),
        in_specs=[pl.BlockSpec(memory_space=pltpu.SMEM)] + [VMEM] * 5,
        out_specs=VMEM,
        scratch_shapes=[pltpu.VMEM((64, 4096), BF16)],
        compiler_params=pltpu.CompilerParams(vmem_limit_bytes=32 << 20),
        cost_estimate=pl.CostEstimate(flops=1 << 30, bytes_accessed=4 << 20, transcendentals=0),
    )(table, x, weights, far, own, right)


def gather_sum(tab_ref, in_ref, acc):
    acc[...] = jnp.zeros_like(acc)
    for b in range(32):
        acc[tab_ref[b]] += in_ref[b].astype(F32)


def segment_kernel(tab_ref, in_ref, out_ref, acc):
    gather_sum(tab_ref, in_ref, acc)
    out_ref[...] = acc[...].astype(BF16)


def segment_sum(table, parts):
    return pl.pallas_call(
        segment_kernel,
        name="segments",
        out_shape=jax.ShapeDtypeStruct((32, ROWS, 128), BF16),
        in_specs=[pl.BlockSpec(memory_space=pltpu.SMEM), VMEM],
        out_specs=VMEM,
        scratch_shapes=[pltpu.VMEM((32, ROWS, 128), F32)],
    )(table, parts)


def adapter_kernel(tab_ref, in_ref, down_ref, up_ref, acc):
    gather_sum(tab_ref, in_ref, acc)
    down_ref[...] = acc[:16, :64, :]
    for r in range(2):
        for c in range(8):
            up_ref[:, r, 128 * c : 128 * (c + 1)] = acc[:16, 64 + 8 * r + c, :]


def adapter_sum(table, parts):
    return pl.pallas_call(
        adapter_kernel,
        name="adapters",
        out_shape=(
            jax.ShapeDtypeStruct((16, 64, 128), F32),
            jax.ShapeDtypeStruct((16, 2, 1024), F32),
        ),
        in_specs=[pl.BlockSpec(memory_space=pltpu.SMEM), VMEM],
        out_specs=(VMEM, VMEM),
        scratch_shapes=[pltpu.VMEM((24, ROWS, 128), F32)],
    )(table, parts)


def exchange(value, axis, groups=None):
    return lax.all_to_all(value, axis, 0, 0, axis_index_groups=groups, tiled=True)


def row_shift(value, step):
    pairs = [
        (8 * x + 2 * q + p, 8 * x + 2 * ((q + step) % 4) + p)
        for x in range(4)
        for q in range(4)
        for p in range(2)
    ]
    return lax.ppermute(value, "seq", pairs)


def rows_gather(value, y2):
    return jnp.concatenate([value] + [row_shift(value, n) for n in (1, 2, 3)], axis=0)


def rows_sum(value, y2):
    total = lax.dynamic_index_in_dim(value, y2, 0, keepdims=False).astype(F32)
    for n in (1, 2, 3):
        piece = lax.dynamic_index_in_dim(value, (y2 + n) % 4, 0, keepdims=False)
        total += row_shift(piece, n).astype(F32)
    return total.astype(BF16)


def local(x, q, k, g, down_weight, up_weight, seg_adapter, seg_blocks, row_index):
    group = lax.axis_index("grp")
    place = lax.axis_index("seq")
    residents = down_weight.shape[0]
    i32 = jnp.int32

    own_weights = jnp.concatenate([down_weight, up_weight.reshape(residents, 16, 128)], axis=1)
    gathered = lax.all_gather(own_weights, "grp", axis=0, tiled=True)

    sent = pack(q, g, k)
    received = exchange(sent, "seq", COLUMN)

    ids = jnp.arange(row_index.shape[0], dtype=i32)
    slot_of = jnp.sum(jnp.where(seg_adapter[:, :, None] == ids, row_index, 0), axis=2)
    owner = slot_of // residents
    inner = slot_of % residents
    order = jnp.arange(16, dtype=i32)
    earlier = order[:, None] > order[None, :]
    rank = jnp.sum(((owner[:, :, None] == owner[:, None, :]) & earlier).astype(i32), axis=2)
    mine = owner == group
    target = jnp.stack(
        [jnp.min(jnp.where(mine & (rank == c), inner, 16), axis=1) for c in range(CAP)], axis=1
    ).reshape(32)

    counts = lax.dynamic_index_in_dim(seg_blocks, group, 0, keepdims=False)
    ends = jnp.sum(jnp.where(order[:, None] >= order[None, :], counts[None, :], 0), axis=1)
    starts = ends - counts
    blocks = jnp.arange(32, dtype=i32)
    inside = (blocks[:, None] >= starts[None, :]) & (blocks[:, None] < ends[None, :])
    own_slots = lax.dynamic_index_in_dim(slot_of, group, 0, keepdims=False)
    own_places = lax.dynamic_index_in_dim(owner * CAP + rank, group, 0, keepdims=False)
    block_slot = jnp.sum(jnp.where(inside, own_slots[None, :], 0), axis=1)
    block_place = jnp.sum(jnp.where(inside, own_places[None, :], 0), axis=1)
    long_start = jnp.sum(jnp.where(counts == LONG, starts, 0))
    pair_start = jnp.sum(jnp.where(counts == 2, starts, 0))
    flags = jnp.stack(
        [
            place == pair_start + 1,
            place == pair_start,
            (place >= long_start) & (place < long_start + LONG),
        ]
    ).astype(i32)

    y2 = (place % 8) // 2
    four = jnp.arange(4, dtype=i32)
    residue = 8 * (four // 2) + 2 * y2 + four % 2
    high = (residue < long_start).astype(i32)
    source = four + 4 * high
    sixteen = (long_start + order) % 16
    within = sixteen // 8 * 2 + sixteen % 2
    home = (sixteen % 8) // 2
    table = jnp.concatenate(
        [source, (residue - long_start) % 16, (y2 - home) % 4 * 4 + within, home * 4 + within]
    )

    halves = received.reshape(2, 4, 128, 1152)[:, :, :, 1024:]
    long_keys = jnp.where(high[:, None, None] > 0, halves[1], halves[0])
    keys = rows_gather(long_keys, y2)

    picked, keys = lax.optimization_barrier((pick(block_slot, gathered), keys))
    weights = exchange(picked, "seq")
    left = lax.ppermute(k, "seq", [(b, b + 1) for b in range(31)])
    own_value, prev_value = short_attention(flags, q, g, k, left)
    right = lax.ppermute(prev_value, "seq", [(b + 1, b) for b in range(31)])

    partial = long_attention(table, received, keys)
    partial, weights, own_value, right = lax.optimization_barrier(
        (partial, weights, own_value, right)
    )
    head_value = rows_sum(partial.reshape(4, 4, 128, 128), y2)
    far = exchange(jnp.concatenate([head_value, head_value], axis=0), "seq", COLUMN)

    parts = exchange(terms(flags, x, weights, far, own_value, right), "seq")
    sums = exchange(segment_sum(block_place, parts), "grp")
    return adapter_sum(target, sums)


def solution(mesh):
    rows = P(("grp", "seq"), None)
    return jax.shard_map(
        local,
        mesh=mesh,
        in_specs=(rows,) * 4 + (P("grp", None, "seq"), P("grp", "seq", None)) + (P(),) * 3,
        out_specs=(P("grp", None, "seq"), P("grp", "seq", None)),
        check_vma=False,
    )
```

time: 594 us -> 220 us (0.37)
  waiting for transfers between devices: 322 us -> 50.2 us
  matrix products: 60.2 us -> 0 us
  local copies, waits for them, and re-layouts: 38.2 us -> 5.75 us
  Pallas kernels: 0 us -> 32.4 us
  starting transfers between devices: 100 us -> 69.9 us
  blocking collectives: 39.6 us -> 32 us
    reduce_scatter x1 -> x0, waiting for transfers between devices: 177 us -> none  [local(): lax.psum_scatter(jnp.einsum('jyw,jaw->jya', token_rows, block_down_weight...]
    all_to_all x11 -> x3, waiting for transfers between devices: 145 us -> 37.4 us  [exchange(): lax.all_to_all(value, axis, 0, 0, axis_index_groups=groups, tiled=True)]
    all_to_all x11 -> x3, starting transfers between devices: 99.8 us -> 35.6 us  [exchange(): lax.all_to_all(value, axis, 0, 0, axis_index_groups=groups, tiled=True)]
    dot_general x28 -> x0, matrix products: 60.2 us -> none  [the longest x8 30.3 us: one_block(): jnp.dot(probabilities.T, grad_block, preferred_element_type=jnp.float32)]
    all_gather x1 -> x0, blocking collectives: 39.6 us -> none  [local(): lax.all_gather(backward_rank_part.reshape(tokens_here, rank_overall), 'se...]
    ppermute x0 -> x8, starting transfers between devices: none -> 34.3 us  [the longest x6 28.9 us: row_shift(): return lax.ppermute(value, 'seq', pairs)]
    pallas_call x0 -> x7, Pallas kernels: none -> 32.4 us  [the longest x1 10.4 us: long_attention(): pl.pallas_call(long_kernel, name='long', out_shape=jax.ShapeDtypeStruct((...]
    all_to_all x0 -> x2, blocking collectives: none -> 32 us  [exchange(): lax.all_to_all(value, axis, 0, 0, axis_index_groups=groups, tiled=True)]
  transfers between devices with their start and end apart: 12 -> 12, of which waited for: 9 -> 6; matrix products, arithmetic and copies ran while one was open for 17% -> 5% of each run, Pallas kernels for 0% -> 12%
where the time goes in v1:
time: 220 us; the launch traced here: 219 us
  starting transfers between devices  69.9 us (32%)
  waiting for transfers between devices  50.2 us (23%)
  Pallas kernels  32.4 us (15%)
  blocking collectives  32 us (15%)
  between operations  16.9 us (8%)
  other arithmetic  11.8 us (5%)
  local copies, waits for them, and re-layouts  5.75 us (3%)
    all_to_all x3, waiting for transfers between devices, exchange(): lax.all_to_all(value, axis, 0, 0, axis_index_groups=groups, tiled=True)  37.4 us
    all_to_all x3, starting transfers between devices, exchange(): lax.all_to_all(value, axis, 0, 0, axis_index_groups=groups, tiled=True)  35.6 us
    all_to_all x2, blocking collectives, exchange(): lax.all_to_all(value, axis, 0, 0, axis_index_groups=groups, tiled=True)  32 us
    ppermute x6, starting transfers between devices, row_shift(): return lax.ppermute(value, 'seq', pairs)  28.9 us
    ppermute x6, waiting for transfers between devices, row_shift(): return lax.ppermute(value, 'seq', pairs)  12.7 us
    pallas_call x1, Pallas kernels, long_attention(): pl.pallas_call(long_kernel, name='long', out_shape=jax.ShapeDtypeStruct((...  10.4 us
    pallas_call x1, Pallas kernels, short_attention(): pl.pallas_call(short_kernel, name='short', out_shape=(jax.ShapeDtypeStruc...  8.05 us
  transfers between devices with their start and end apart: 12, of which 6 were waited for; matrix products, arithmetic and copies ran while one was open for 5% of the time, Pallas kernels for 12%

profile of v1, /device:TPU:1, one launch (start us, length us, event | category | flops | bytes accessed | tf_op | source)
XLA Modules:
  0.0 218.9 jit_solution(10540602642926903601)
XLA Ops:
  8.1 1.7 pad_maximum_fusion.1
  9.8 3.8 %pack.1 = bf16[8,128,1152]{2,1,0:T(8,128)(2,1)} custom-call(bf16[128,4096]{1,0:T(8,128)(2,1)} %q_ref.3, bf16[128,4096]{1,0:T(8,128)(2,1)} %g_ref.3, bf16[128,1024]{1,0:T(8,128)(2,1)} %k_ref.3), custom_call_target="tpu_custom_call" | custom-call | bytes 5242880 | tf_op jit(solution)/shard_map/pack/pallas_call | solution.py:52
  13.7 6.0 %all-to-all-start = ((bf16[8,128,1152]{2,1,0:T(8,128)(2,1)}), bf16[8,128,1152]{2,1,0:T(8,128)(2,1)S(1)}, u32[]{:S(2)}, u32[]{:S(2)}) async-start(bf16[8,128,1152]{2,1,0:T(8,128)(2,1)} %pack.1), calls=%async_computation | async-start | bytes 4718592 | tf_op jit(solution)/shard_map/all_to_all | solution.py:304
  19.7 4.1 %collective-permute-start.3 = (bf16[128,1024]{1,0:T(8,128)(2,1)}, bf16[128,1024]{1,0:T(8,128)(2,1)}, u32[]{:S(2)}, u32[]{:S(2)}) collective-permute-start(bf16[128,1024]{1,0:T(8,128)(2,1)} %k_ref.3), channel_id=1, source_target_pairs={{0,16},{16,32},{32,48},{48,64},{64,80},{80,96},{96,112},{112,128},... | collective-permute-start | bytes 786440 | tf_op jit(solution)/shard_map/ppermute | solution.py:390
  29.4 18.2 %all-to-all-done.recv_ref = bf16[8,128,1152]{2,1,0:T(8,128)(2,1)S(1)} async-done(((bf16[8,128,1152]{2,1,0:T(8,128)(2,1)}), bf16[8,128,1152]{2,1,0:T(8,128)(2,1)S(1)}, u32[]{:S(2)}, u32[]{:S(2)}) %all-to-all-start) | async-done | bytes 2359328 | tf_op jit(solution)/shard_map/all_to_all | solution.py:304
  47.8 5.9 %collective-permute-start.2 = (bf16[4,128,128]{2,1,0:T(8,128)(2,1)S(1)}, bf16[4,128,128]{2,1,0:T(8,128)(2,1)S(1)}, u32[]{:S(2)}, u32[]{:S(2)}) collective-permute-start(bf16[4,128,128]{2,1,0:T(8,128)(2,1)S(1)} %fusion.3), channel_id=1, source_target_pairs={{0,96},{16,112},{32,0},{48,16},{64,32},{80,48},{96,64},{112,80},{1... | collective-permute-start | bytes 393224 | tf_op jit(solution)/shard_map/ppermute | solution.py:314
  53.6 4.4 %collective-permute-start.1 = (bf16[4,128,128]{2,1,0:T(8,128)(2,1)S(1)}, bf16[4,128,128]{2,1,0:T(8,128)(2,1)S(1)}, u32[]{:S(2)}, u32[]{:S(2)}) collective-permute-start(bf16[4,128,128]{2,1,0:T(8,128)(2,1)S(1)} %fusion.3), channel_id=1, source_target_pairs={{0,64},{16,80},{32,96},{48,112},{64,0},{80,16},{96,32},{112,48},{1... | collective-permute-start | bytes 393224 | tf_op jit(solution)/shard_map/ppermute | solution.py:314
  58.1 3.3 %collective-permute-start = (bf16[4,128,128]{2,1,0:T(8,128)(2,1)S(1)}, bf16[4,128,128]{2,1,0:T(8,128)(2,1)S(1)}, u32[]{:S(2)}, u32[]{:S(2)}) collective-permute-start(bf16[4,128,128]{2,1,0:T(8,128)(2,1)S(1)} %fusion.3), channel_id=1, source_target_pairs={{0,32},{16,48},{32,64},{48,80},{64,96},{80,112},{96,0},{112,16},{1... | collective-permute-start | bytes 393224 | tf_op jit(solution)/shard_map/ppermute | solution.py:314
  63.3 2.7 %collective-permute-done = bf16[4,128,128]{2,1,0:T(8,128)(2,1)S(1)} collective-permute-done((bf16[4,128,128]{2,1,0:T(8,128)(2,1)S(1)}, bf16[4,128,128]{2,1,0:T(8,128)(2,1)S(1)}, u32[]{:S(2)}, u32[]{:S(2)}) %collective-permute-start) | collective-permute-done | bytes 131104 | tf_op jit(solution)/shard_map/ppermute | solution.py:314
  66.1 3.2 %pick.1 = bf16[32,80,128]{2,1,0:T(8,128)(2,1)} custom-call(s32[32]{0:T(128)} %get-tuple-element.20.slot_ref, bf16[256,80,128]{2,1,0:T(8,128)(2,1)} %all-gather.2.cloned.1.call-done.all_ref), custom_call_target="tpu_custom_call" | custom-call | bytes 1048576 | tf_op jit(solution)/shard_map/pick/pallas_call | solution.py:78
  69.3 12.2 %all-to-all-start.1 = ((bf16[32,80,128]{2,1,0:T(8,128)(2,1)}), bf16[32,80,128]{2,1,0:T(8,128)(2,1)S(1)}, u32[]{:S(2)}, u32[]{:S(2)}) async-start(bf16[32,80,128]{2,1,0:T(8,128)(2,1)} %pick.1), calls=%async_computation.1 | async-start | bytes 1310720 | tf_op jit(solution)/shard_map/all_to_all | solution.py:304
  87.4 8.0 %short.1 = (f32[128,1024]{1,0:T(8,128)}, bf16[128,1024]{1,0:T(8,128)(2,1)}) custom-call(s32[3]{0:T(128)} %add_convert_fusion.tab_ref, bf16[128,4096]{1,0:T(8,128)(2,1)} %q_ref.3, bf16[128,4096]{1,0:T(8,128)(2,1)} %g_ref.3, bf16[128,1024]{1,0:T(8,128)(2,1)} %k_ref.3, bf16[128,1024]{1,0:T(8,128)(2,1)} %collective-permute-done.3.left_ref), custom_call_target="tpu_custom_call" | custom-call | flops 3221225472 | bytes 4194304 | tf_op jit(solution)/shard_map/short/pallas_call | solution.py:197
  96.7 10.4 %long.1 = bf16[16,128,128]{2,1,0:T(8,128)(2,1)S(1)} custom-call(s32[40]{0:T(128)S(1)} %pad_add_fusion.1.tab_ref, bf16[8,128,1152]{2,1,0:T(8,128)(2,1)S(1)} %all-to-all-done.recv_ref, bf16[16,128,128]{2,1,0:T(8,128)(2,1)S(1)} %pad_maximum_fusion.key_ref), custom_call_target="tpu_custom_call" | custom-call | flops 6442450944 | bytes 3145728 | tf_op jit(solution)/shard_map/long/pallas_call | solution.py:147
  109.8 2.8 %collective-permute-start.5 = (bf16[4,128,128]{2,1,0:T(8,128)(2,1)S(1)}, bf16[4,128,128]{2,1,0:T(8,128)(2,1)S(1)}, u32[]{:S(2)}, u32[]{:S(2)}) collective-permute-start(bf16[4,128,128]{2,1,0:T(8,128)(2,1)S(1)} %get-tuple-element.26), channel_id=1, source_target_pairs={{0,32},{16,48},{32,64},{48,80},{64,96},{80,112},{96,0},{112,16},{1... | collective-permute-start | bytes 393224 | tf_op jit(solution)/shard_map/ppermute | solution.py:314
  112.6 8.3 %collective-permute-start.7 = (bf16[4,128,128]{2,1,0:T(8,128)(2,1)S(1)}, bf16[4,128,128]{2,1,0:T(8,128)(2,1)S(1)}, u32[]{:S(2)}, u32[]{:S(2)}) collective-permute-start(bf16[4,128,128]{2,1,0:T(8,128)(2,1)S(1)} %get-tuple-element.27), channel_id=1, source_target_pairs={{0,96},{16,112},{32,0},{48,16},{64,32},{80,48},{96,64},{112,80},{1... | collective-permute-start | bytes 393224 | tf_op jit(solution)/shard_map/ppermute | solution.py:314
  120.9 4.3 %collective-permute-start.6 = (bf16[4,128,128]{2,1,0:T(8,128)(2,1)S(1)}, bf16[4,128,128]{2,1,0:T(8,128)(2,1)S(1)}, u32[]{:S(2)}, u32[]{:S(2)}) collective-permute-start(bf16[4,128,128]{2,1,0:T(8,128)(2,1)S(1)} %get-tuple-element.28), channel_id=1, source_target_pairs={{0,64},{16,80},{32,96},{48,112},{64,0},{80,16},{96,32},{112,48},{1... | collective-permute-start | bytes 393224 | tf_op jit(solution)/shard_map/ppermute | solution.py:314
  126.7 7.2 %collective-permute-done.6 = bf16[4,128,128]{2,1,0:T(8,128)(2,1)S(1)} collective-permute-done((bf16[4,128,128]{2,1,0:T(8,128)(2,1)S(1)}, bf16[4,128,128]{2,1,0:T(8,128)(2,1)S(1)}, u32[]{:S(2)}, u32[]{:S(2)}) %collective-permute-start.6) | collective-permute-done | bytes 131104 | tf_op jit(solution)/shard_map/ppermute | solution.py:314
  135.0 12.8 %all_to_all.25.far_ref = bf16[8,128,128]{2,1,0:T(8,128)(2,1)S(1)} all-to-all(bf16[8,128,128]{2,1,0:T(8,128)(2,1)S(1)} %pad_maximum_fusion.2), channel_id=1, replica_groups={{0,16,128,144,256,272,384,400},{32,48,160,176,288,304,416,432},{64,80,1..., dimensions={0} | all-to-all | bytes 524288 | tf_op jit(solution)/shard_map/all_to_all | solution.py:304
  147.8 2.2 %terms.1 = bf16[32,80,128]{2,1,0:T(8,128)(2,1)S(1)} custom-call(s32[3]{0:T(128)S(1)} %copy-done.1, bf16[128,4096]{1,0:T(8,128)(2,1)S(1)} %copy-done.2, bf16[32,80,128]{2,1,0:T(8,128)(2,1)S(1)} %all-to-all-done.1.w_ref, bf16[8,128,128]{2,1,0:T(8,128)(2,1)S(1)} %all_to_all.25.far_ref, f32[128,1024]{1,0:T(8,128)S(1)} %copy-done.5, bf16[128,1024]{1,0:T(8,128)(2,1)S(1)} %copy-done.4), custom_call_target="tpu_custom_call" | custom-call | flops 1073741824 | bytes 4194304 | tf_op jit(solution)/shard_map/terms/pallas_call | solution.py:247
  150.0 19.2 %all_to_all.26.in_ref = bf16[32,80,128]{2,1,0:T(8,128)(2,1)} all-to-all(bf16[32,80,128]{2,1,0:T(8,128)(2,1)S(1)} %terms.1), channel_id=1, replica_groups=mesh['seq'=32,'grp'=16] {'seq'}, dimensions={0} | all-to-all | bytes 1310720 | tf_op jit(solution)/shard_map/all_to_all | solution.py:304
  169.2 2.3 %segments.1 = bf16[32,80,128]{2,1,0:T(8,128)(2,1)} custom-call(s32[32]{0:T(128)} %get-tuple-element.21.tab_ref, bf16[32,80,128]{2,1,0:T(8,128)(2,1)} %all_to_all.26.in_ref), custom_call_target="tpu_custom_call" | custom-call | tf_op jit(solution)/shard_map/segments/pallas_call | solution.py:271
  171.5 17.3 %all-to-all-start.4 = ((bf16[32,80,128]{2,1,0:T(8,128)(2,1)}), bf16[32,80,128]{2,1,0:T(8,128)(2,1)S(1)}, u32[]{:S(2)}, u32[]{:S(2)}) async-start(bf16[32,80,128]{2,1,0:T(8,128)(2,1)} %segments.1), calls=%async_computation.4 | async-start | bytes 1310720 | tf_op jit(solution)/shard_map/all_to_all | solution.py:304
  189.7 19.2 %all-to-all-done.4.in_ref = bf16[32,80,128]{2,1,0:T(8,128)(2,1)S(1)} async-done(((bf16[32,80,128]{2,1,0:T(8,128)(2,1)}), bf16[32,80,128]{2,1,0:T(8,128)(2,1)S(1)}, u32[]{:S(2)}, u32[]{:S(2)}) %all-to-all-start.4) | async-done | bytes 655392 | tf_op jit(solution)/shard_map/all_to_all | solution.py:304
  209.7 2.3 %adapters.1 = (f32[16,64,128]{2,1,0:T(8,128)}, f32[16,2,1024]{2,1,0:T(2,128)}) custom-call(s32[32]{0:T(128)} %reshape.94.tab_ref, bf16[32,80,128]{2,1,0:T(8,128)(2,1)} %copy-done.6), custom_call_target="tpu_custom_call" | custom-call | tf_op jit(solution)/shard_map/adapters/pallas_call | solution.py:290
  (58 shorter events, 20.0 us)
Async XLA Ops:
  7.2 58.9 %all-gather.2.cloned.1.call-start = ((), (), s32[]{:S(2)}) async-start(), calls=%async_computation.5 | async-start | bytes 5570560 | tf_op jit(solution)/shard_map/all_gather | solution.py:336
  13.7 14.2 %copy-start.9 = (s32[16,16]{1,0:T(8,128)S(1)}, s32[16,16]{1,0:T(8,128)}, u32[]{:S(2)}) copy-start(s32[16,16]{1,0:T(8,128)} %param.15) | copy-start | bytes 3076
  13.7 14.2 %copy-start.10 = (s32[256]{0:T(256)S(1)}, s32[256]{0:T(256)}, u32[]{:S(2)}) copy-start(s32[256]{0:T(256)} %param.17) | copy-start | bytes 3076
  13.7 34.0 %all-to-all-start = ((bf16[8,128,1152]{2,1,0:T(8,128)(2,1)}), bf16[8,128,1152]{2,1,0:T(8,128)(2,1)S(1)}, u32[]{:S(2)}, u32[]{:S(2)}) async-start(bf16[8,128,1152]{2,1,0:T(8,128)(2,1)} %pack.1), calls=%async_computation | async-start | bytes 4718592 | tf_op jit(solution)/shard_map/all_to_all | solution.py:304
  19.7 67.7 %collective-permute-start.3 = (bf16[128,1024]{1,0:T(8,128)(2,1)}, bf16[128,1024]{1,0:T(8,128)(2,1)}, u32[]{:S(2)}, u32[]{:S(2)}) collective-permute-start(bf16[128,1024]{1,0:T(8,128)(2,1)} %k_ref.3), channel_id=1, source_target_pairs={{0,16},{16,32},{32,48},{48,64},{64,80},{80,96},{96,112},{112,128},... | collective-permute-start | bytes 786440 | tf_op jit(solution)/shard_map/ppermute | solution.py:390
  28.7 40.6 %copy-start.7 = (s32[16,16]{1,0:T(8,128)}, s32[16,16]{1,0:T(8,128)S(1)}, u32[]{:S(2)}) copy-start(s32[16,16]{1,0:T(8,128)S(1)} %convert_reduce_fusion) | copy-start | bytes 3076
  47.8 14.3 %collective-permute-start.2 = (bf16[4,128,128]{2,1,0:T(8,128)(2,1)S(1)}, bf16[4,128,128]{2,1,0:T(8,128)(2,1)S(1)}, u32[]{:S(2)}, u32[]{:S(2)}) collective-permute-start(bf16[4,128,128]{2,1,0:T(8,128)(2,1)S(1)} %fusion.3), channel_id=1, source_target_pairs={{0,96},{16,112},{32,0},{48,16},{64,32},{80,48},{96,64},{112,80},{1... | collective-permute-start | bytes 393224 | tf_op jit(solution)/shard_map/ppermute | solution.py:314
  53.6 9.6 %collective-permute-start.1 = (bf16[4,128,128]{2,1,0:T(8,128)(2,1)S(1)}, bf16[4,128,128]{2,1,0:T(8,128)(2,1)S(1)}, u32[]{:S(2)}, u32[]{:S(2)}) collective-permute-start(bf16[4,128,128]{2,1,0:T(8,128)(2,1)S(1)} %fusion.3), channel_id=1, source_target_pairs={{0,64},{16,80},{32,96},{48,112},{64,0},{80,16},{96,32},{112,48},{1... | collective-permute-start | bytes 393224 | tf_op jit(solution)/shard_map/ppermute | solution.py:314
  58.1 7.9 %collective-permute-start = (bf16[4,128,128]{2,1,0:T(8,128)(2,1)S(1)}, bf16[4,128,128]{2,1,0:T(8,128)(2,1)S(1)}, u32[]{:S(2)}, u32[]{:S(2)}) collective-permute-start(bf16[4,128,128]{2,1,0:T(8,128)(2,1)S(1)} %fusion.3), channel_id=1, source_target_pairs={{0,32},{16,48},{32,64},{48,80},{64,96},{80,112},{96,0},{112,16},{1... | collective-permute-start | bytes 393224 | tf_op jit(solution)/shard_map/ppermute | solution.py:314
  69.3 39.3 %all-to-all-start.1 = ((bf16[32,80,128]{2,1,0:T(8,128)(2,1)}), bf16[32,80,128]{2,1,0:T(8,128)(2,1)S(1)}, u32[]{:S(2)}, u32[]{:S(2)}) async-start(bf16[32,80,128]{2,1,0:T(8,128)(2,1)} %pick.1), calls=%async_computation.1 | async-start | bytes 1310720 | tf_op jit(solution)/shard_map/all_to_all | solution.py:304
  95.4 12.5 %collective-permute-start.4 = (bf16[128,1024]{1,0:T(8,128)(2,1)}, bf16[128,1024]{1,0:T(8,128)(2,1)S(1)}, u32[]{:S(2)}, u32[]{:S(2)}) collective-permute-start(bf16[128,1024]{1,0:T(8,128)(2,1)} %get-tuple-element.13), channel_id=1, source_target_pairs={{16,0},{32,16},{48,32},{64,48},{80,64},{96,80},{112,96},{128,112},... | collective-permute-start | bytes 786440 | tf_op jit(solution)/shard_map/ppermute | solution.py:392
  107.1 0.8 copy-start
  107.9 39.9 %copy-start.1 = (s32[3]{0:T(128)S(1)}, s32[3]{0:T(128)}, u32[]{:S(2)}) copy-start(s32[3]{0:T(128)} %add_convert_fusion.tab_ref) | copy-start | bytes 40
  107.9 39.9 %copy-start.2 = (bf16[128,4096]{1,0:T(8,128)(2,1)S(1)}, bf16[128,4096]{1,0:T(8,128)(2,1)}, u32[]{:S(2)}) copy-start(bf16[128,4096]{1,0:T(8,128)(2,1)} %x_ref.1) | copy-start | bytes 3145732
  107.9 39.9 %copy-start.5 = (f32[128,1024]{1,0:T(8,128)S(1)}, f32[128,1024]{1,0:T(8,128)}, u32[]{:S(2)}) copy-start(f32[128,1024]{1,0:T(8,128)} %get-tuple-element.16.own_ref) | copy-start | bytes 1572868
  107.9 0.7 copy-start.3
  108.6 39.1 %copy-start.4 = (bf16[128,1024]{1,0:T(8,128)(2,1)S(1)}, bf16[128,1024]{1,0:T(8,128)(2,1)}, u32[]{:S(2)}) copy-start(bf16[128,1024]{1,0:T(8,128)(2,1)} %copy-done.3) | copy-start | bytes 786436
  109.8 15.4 %collective-permute-start.5 = (bf16[4,128,128]{2,1,0:T(8,128)(2,1)S(1)}, bf16[4,128,128]{2,1,0:T(8,128)(2,1)S(1)}, u32[]{:S(2)}, u32[]{:S(2)}) collective-permute-start(bf16[4,128,128]{2,1,0:T(8,128)(2,1)S(1)} %get-tuple-element.26), channel_id=1, source_target_pairs={{0,32},{16,48},{32,64},{48,80},{64,96},{80,112},{96,0},{112,16},{1... | collective-permute-start | bytes 393224 | tf_op jit(solution)/shard_map/ppermute | solution.py:314
  112.6 14.1 %collective-permute-start.7 = (bf16[4,128,128]{2,1,0:T(8,128)(2,1)S(1)}, bf16[4,128,128]{2,1,0:T(8,128)(2,1)S(1)}, u32[]{:S(2)}, u32[]{:S(2)}) collective-permute-start(bf16[4,128,128]{2,1,0:T(8,128)(2,1)S(1)} %get-tuple-element.27), channel_id=1, source_target_pairs={{0,96},{16,112},{32,0},{48,16},{64,32},{80,48},{96,64},{112,80},{1... | collective-permute-start | bytes 393224 | tf_op jit(solution)/shard_map/ppermute | solution.py:314
  120.9 13.1 %collective-permute-start.6 = (bf16[4,128,128]{2,1,0:T(8,128)(2,1)S(1)}, bf16[4,128,128]{2,1,0:T(8,128)(2,1)S(1)}, u32[]{:S(2)}, u32[]{:S(2)}) collective-permute-start(bf16[4,128,128]{2,1,0:T(8,128)(2,1)S(1)} %get-tuple-element.28), channel_id=1, source_target_pairs={{0,64},{16,80},{32,96},{48,112},{64,0},{80,16},{96,32},{112,48},{1... | collective-permute-start | bytes 393224 | tf_op jit(solution)/shard_map/ppermute | solution.py:314
  150.0 38.8 %copy-start.8 = (s32[16,16]{1,0:T(8,128)S(1)}, s32[16,16]{1,0:T(8,128)}, u32[]{:S(2)}) copy-start(s32[16,16]{1,0:T(8,128)} %copy-done.7) | copy-start | bytes 3076
  171.5 37.4 %all-to-all-start.4 = ((bf16[32,80,128]{2,1,0:T(8,128)(2,1)}), bf16[32,80,128]{2,1,0:T(8,128)(2,1)S(1)}, u32[]{:S(2)}, u32[]{:S(2)}) async-start(bf16[32,80,128]{2,1,0:T(8,128)(2,1)} %segments.1), calls=%async_computation.4 | async-start | bytes 1310720 | tf_op jit(solution)/shard_map/all_to_all | solution.py:304
  208.9 0.8 copy-start.6
Sparse Core Ops, SparseCore 0:
  10.7 52.6 all-gather.1

commit v2 on v1

v2 whole, which is shorter than its diff:
```python
import math

import jax
import jax.numpy as jnp
from jax import lax
from jax.experimental import pallas as pl
from jax.experimental.pallas import tpu as pltpu
from jax.sharding import PartitionSpec as P

HEAD_DIM = 128
BLOCK = 128
LONG = 16
CAP = 2
ROWS = 80
NEG = -1e30
FACTOR = 1.0 / math.sqrt(HEAD_DIM)

COLUMN = [[8 * x + 2 * q + p for x in range(4) for p in range(2)] for q in range(4)]

VMEM = pl.BlockSpec(memory_space=pltpu.VMEM)
SMEM = pl.BlockSpec(memory_space=pltpu.SMEM)
F32 = jnp.float32
BF16 = jnp.bfloat16


def dot_nt(a, b):
    return lax.dot_general(a, b, (((1,), (1,)), ((), ())), preferred_element_type=F32)


def dot_tn(a, b):
    return lax.dot_general(a, b, (((0,), (0,)), ((), ())), preferred_element_type=F32)


def dot_nn(a, b):
    return jnp.dot(a, b, preferred_element_type=F32)


def stack_heads(rows):
    return jnp.concatenate([rows[:, h * 128 : (h + 1) * 128] for h in range(4)], axis=0)


def pack_kernel(q_ref, g_ref, k_ref, out_ref):
    for h in range(8):
        out_ref[h, :, :512] = q_ref[:, 512 * h : 512 * (h + 1)]
        out_ref[h, :, 512:1024] = g_ref[:, 512 * h : 512 * (h + 1)]
        out_ref[h, :, 1024:] = k_ref[:, 128 * h : 128 * (h + 1)]


def pack(q, g, k):
    def rows(width):
        return pl.BlockSpec((32, width), lambda i: (i, 0))

    return pl.pallas_call(
        pack_kernel,
        name="pack",
        out_shape=jax.ShapeDtypeStruct((8, 128, 1152), BF16),
        grid=(4,),
        in_specs=[rows(4096), rows(4096), rows(1024)],
        out_specs=pl.BlockSpec((8, 32, 1152), lambda i: (0, i, 0)),
        cost_estimate=pl.CostEstimate(flops=0, bytes_accessed=5 << 20, transcendentals=0),
    )(q, g, k)


def choose_kernel(tab_ref, down_ref, up_ref, out_ref):
    for n in range(32):
        row = jnp.minimum(tab_ref[n], 15)
        out_ref[n, :64, :] = down_ref[row]
        out_ref[n, 64:, :] = up_ref[row]


def choose(table, down, up):
    return pl.pallas_call(
        choose_kernel,
        name="choose",
        out_shape=jax.ShapeDtypeStruct((32, ROWS, 128), BF16),
        in_specs=[SMEM, VMEM, VMEM],
        out_specs=VMEM,
        cost_estimate=pl.CostEstimate(flops=0, bytes_accessed=1 << 20, transcendentals=0),
    )(table, down, up)


def pick_kernel(tab_ref, in_ref, out_ref):
    for b in range(32):
        out_ref[b] = in_ref[tab_ref[b]]


def pick(table, fetched):
    return pl.pallas_call(
        pick_kernel,
        name="pick",
        out_shape=jax.ShapeDtypeStruct((32, ROWS, 128), BF16),
        in_specs=[SMEM, VMEM],
        out_specs=VMEM,
        cost_estimate=pl.CostEstimate(flops=0, bytes_accessed=1 << 20, transcendentals=0),
    )(table, fetched)


def long_kernel(tab_ref, own_ref, key_ref, out_ref, keys, acc, sc):
    i = pl.program_id(0)

    @pl.when(i == 0)
    def _():
        acc[...] = jnp.zeros_like(acc)
        for j in range(LONG + 1):
            keys[pl.ds(128 * j, 128), :] = key_ref[tab_ref[10 + j]]

    pos = tab_ref[5 + i]
    last = pos // 2
    base = jnp.where(i == 4, LONG * 128, 0)

    @pl.when(pos >= 0)
    def _():
        own = own_ref[0]
        queries = stack_heads(own[:, :512])
        grads = stack_heads(own[:, 512:1024])

        @pl.when(i == 4)
        def _():
            keys[pl.ds(2176, 128), :] = own[:, 1024:]

        def rows(c):
            return pl.ds(pl.multiple_of(base + c * 256, 256), 256)

        def scores(c):
            return dot_nt(keys[rows(c), :], queries) * FACTOR

        def fold(s):
            return jnp.max(s.reshape(32, 8, 512), axis=0)

        def first(c, top):
            s = scores(c)
            sc[c] = s
            return jnp.maximum(top, fold(s))

        s = scores(last)
        key_at = lax.broadcasted_iota(jnp.int32, (256, 512), 0) + last * 256
        query_at = (lax.broadcasted_iota(jnp.int32, (256, 512), 1) & 127) + pos * 128
        s = jnp.where(key_at <= query_at, s, NEG)
        sc[last] = s
        top = lax.fori_loop(0, last, first, fold(s))
        top = jnp.max(top, axis=0, keepdims=True)

        def second(c, total):
            e = jnp.exp(sc[c] - top)
            sc[c] = e
            return total + jnp.sum(e.reshape(32, 8, 512), axis=0)

        total = lax.fori_loop(0, last + 1, second, jnp.zeros((8, 512), F32))
        inverse = 1.0 / jnp.sum(total, axis=0, keepdims=True)

        def third(c, carry):
            p = (sc[c] * inverse).astype(BF16)
            acc[rows(c), :] += dot_nn(p, grads)
            return carry

        lax.fori_loop(0, last + 1, third, 0)

    @pl.when(i == 4)
    def _():
        for j in range(LONG):
            out_ref[tab_ref[27 + j]] = acc[pl.ds(128 * j, 128), :].astype(BF16)
        shared = acc[2048:2176, :].astype(BF16)
        out_ref[4] = shared
        out_ref[17] = shared
        out_ref[18] = acc[2176:, :].astype(BF16)


def long_attention(table, received, keys):
    def whole(*shape):
        return pl.BlockSpec(shape, lambda i, t: (0,) * len(shape))

    return pl.pallas_call(
        long_kernel,
        name="long",
        out_shape=jax.ShapeDtypeStruct((19, 128, 128), BF16),
        grid_spec=pltpu.PrefetchScalarGridSpec(
            num_scalar_prefetch=1,
            grid=(5,),
            in_specs=[
                pl.BlockSpec((1, 128, 1152), lambda i, t: (t[i], 0, 0)),
                whole(18, 128, 128),
            ],
            out_specs=whole(19, 128, 128),
            scratch_shapes=[
                pltpu.VMEM((2304, 128), BF16),
                pltpu.VMEM((2304, 128), F32),
                pltpu.VMEM((8, 256, 512), F32),
            ],
        ),
        compiler_params=pltpu.CompilerParams(vmem_limit_bytes=32 << 20),
        cost_estimate=pl.CostEstimate(
            flops=6 << 30, bytes_accessed=4 << 20, transcendentals=8 << 20
        ),
    )(table, received, keys)


def short_kernel(q_ref, g_ref, k_ref, out_ref):
    key_at = lax.broadcasted_iota(jnp.int32, (128, 512), 0)
    query_at = lax.broadcasted_iota(jnp.int32, (128, 512), 1) & 127
    s = dot_nt(k_ref[...], stack_heads(q_ref[...])) * FACTOR
    s = jnp.where(key_at <= query_at, s, NEG)
    e = jnp.exp(s - jnp.max(s, axis=0, keepdims=True))
    p = (e * (1.0 / jnp.sum(e, axis=0, keepdims=True))).astype(BF16)
    summed = jnp.zeros((128, 128), F32)
    for h in range(4):
        lanes = slice(h * 128, (h + 1) * 128)
        summed += dot_nn(p[:, lanes], g_ref[:, lanes]).astype(BF16).astype(F32)
    out_ref[...] = summed.astype(BF16)


def short_attention(q, g, k):
    wide = pl.BlockSpec((128, 512), lambda i: (0, i))
    thin = pl.BlockSpec((128, 128), lambda i: (0, i))
    return pl.pallas_call(
        short_kernel,
        name="short",
        out_shape=jax.ShapeDtypeStruct((128, 1024), BF16),
        grid=(8,),
        in_specs=[wide, wide, thin],
        out_specs=thin,
        cost_estimate=pl.CostEstimate(
            flops=3 << 30, bytes_accessed=4 << 20, transcendentals=4 << 20
        ),
    )(q, g, k)


def interleave(transposed):
    row = lax.broadcasted_iota(jnp.int32, (512, 512), 0)
    col = lax.broadcasted_iota(jnp.int32, (512, 512), 1)
    if transposed:
        row, col = col, row
    return (col == (row & 7) * 64 + (row >> 3)).astype(BF16)


def terms_kernel(tab_ref, x_ref, w_ref, far_ref, own_ref, out_ref, down):
    for s in range(32):
        down[:, 128 * s : 128 * (s + 1)] = w_ref[s, :64, :]
    low = dot_nt(x_ref[...], down[...]).astype(BF16)
    up = dot_nn(interleave(True), w_ref[:, 64:, :].reshape(512, 128)).astype(BF16)
    near, wide = tab_ref[0] > 0, tab_ref[1] > 0
    back = jnp.zeros((128, 64), F32)
    up_terms = []
    for c in range(8):
        lanes = slice(c * 128, (c + 1) * 128)
        value = jnp.where(near, own_ref[:, lanes].astype(F32), 0.0)
        value = (value + jnp.where(wide, far_ref[c].astype(F32), 0.0)).astype(BF16)
        back += dot_nt(value, up[64 * c : 64 * (c + 1), :])
        up_terms.append((2.0 * dot_tn(low, value)).astype(BF16))
    mixed = dot_nn(interleave(False), jnp.concatenate(up_terms, axis=0)).astype(BF16)
    out_ref[:, 64:, :] = mixed.reshape(32, 16, 128)
    back = (2.0 * back).astype(BF16)
    for s in range(32):
        out_ref[s, :64, :] = dot_tn(back, x_ref[:, 128 * s : 128 * (s + 1)]).astype(BF16)


def terms(table, x, weights, far, own):
    return pl.pallas_call(
        terms_kernel,
        name="terms",
        out_shape=jax.ShapeDtypeStruct((32, ROWS, 128), BF16),
        in_specs=[SMEM] + [VMEM] * 4,
        out_specs=VMEM,
        scratch_shapes=[pltpu.VMEM((64, 4096), BF16)],
        compiler_params=pltpu.CompilerParams(vmem_limit_bytes=32 << 20),
        cost_estimate=pl.CostEstimate(flops=1 << 30, bytes_accessed=4 << 20, transcendentals=0),
    )(table, x, weights, far, own)


def gather_sum(tab_ref, in_ref, acc):
    acc[...] = jnp.zeros_like(acc)
    for b in range(32):
        acc[tab_ref[b]] += in_ref[b].astype(F32)


def segment_kernel(tab_ref, in_ref, out_ref, acc):
    gather_sum(tab_ref, in_ref, acc)
    out_ref[...] = acc[...].astype(BF16)


def segment_sum(table, parts):
    return pl.pallas_call(
        segment_kernel,
        name="segments",
        out_shape=jax.ShapeDtypeStruct((32, ROWS, 128), BF16),
        in_specs=[SMEM, VMEM],
        out_specs=VMEM,
        scratch_shapes=[pltpu.VMEM((32, ROWS, 128), F32)],
    )(table, parts)


def adapter_kernel(tab_ref, in_ref, down_ref, up_ref, acc):
    gather_sum(tab_ref, in_ref, acc)
    down_ref[...] = acc[:16, :64, :]
    for r in range(2):
        for c in range(8):
            up_ref[:, r, 128 * c : 128 * (c + 1)] = acc[:16, 64 + 8 * r + c, :]


def adapter_sum(table, parts):
    return pl.pallas_call(
        adapter_kernel,
        name="adapters",
        out_shape=(
            jax.ShapeDtypeStruct((16, 64, 128), F32),
            jax.ShapeDtypeStruct((16, 2, 1024), F32),
        ),
        in_specs=[SMEM, VMEM],
        out_specs=(VMEM, VMEM),
        scratch_shapes=[pltpu.VMEM((24, ROWS, 128), F32)],
    )(table, parts)


def exchange(value, axis, groups=None):
    return lax.all_to_all(value, axis, 0, 0, axis_index_groups=groups, tiled=True)


def row_shift(value, step):
    pairs = [
        (8 * x + 2 * q + p, 8 * x + 2 * ((q + step) % 4) + p)
        for x in range(4)
        for q in range(4)
        for p in range(2)
    ]
    return lax.ppermute(value, "seq", pairs)


def local(x, q, k, g, down_weight, up_weight, seg_adapter, seg_blocks, row_index):
    group = lax.axis_index("grp")
    place = lax.axis_index("seq")
    residents = down_weight.shape[0]
    i32 = jnp.int32

    received = exchange(pack(q, g, k), "seq", COLUMN)
    own_value = short_attention(q, g, k)

    ids = jnp.arange(row_index.shape[0], dtype=i32)
    slot_of = jnp.sum(jnp.where(seg_adapter[:, :, None] == ids, row_index, 0), axis=2)
    owner = slot_of // residents
    inner = slot_of % residents
    order = jnp.arange(16, dtype=i32)
    earlier = order[:, None] > order[None, :]
    rank = jnp.sum(((owner[:, :, None] == owner[:, None, :]) & earlier).astype(i32), axis=2)
    mine = owner == group
    target = jnp.stack(
        [jnp.min(jnp.where(mine & (rank == c), inner, 16), axis=1) for c in range(CAP)], axis=1
    ).reshape(32)

    counts = lax.dynamic_index_in_dim(seg_blocks, group, 0, keepdims=False)
    ends = jnp.sum(jnp.where(order[:, None] >= order[None, :], counts[None, :], 0), axis=1)
    starts = ends - counts
    blocks = jnp.arange(32, dtype=i32)
    inside = (blocks[:, None] >= starts[None, :]) & (blocks[:, None] < ends[None, :])
    own_places = lax.dynamic_index_in_dim(owner * CAP + rank, group, 0, keepdims=False)
    block_place = jnp.sum(jnp.where(inside, own_places[None, :], 0), axis=1)
    long_start = jnp.sum(jnp.where(counts == LONG, starts, 0))
    pair_start = jnp.sum(jnp.where(counts == 2, starts, 0))
    counted = jnp.sum(jnp.where(inside, counts[None, :], 0), axis=1)
    counted = lax.dynamic_index_in_dim(counted, place, 0)
    flags = jnp.concatenate([(counted == 1) | (place == pair_start), counted > 1]).astype(i32)

    y2 = (place % 8) // 2
    four = jnp.arange(4, dtype=i32)
    residue = 8 * (four // 2) + 2 * y2 + four % 2
    source = jnp.where(residue < long_start, four + 4, four)
    pair = pair_start + jnp.arange(2, dtype=i32)
    pair_member = pair // 8 * 2 + pair % 2
    pair_row = (pair % 8) // 2
    sixteen = (long_start + order) % 16
    within = sixteen // 8 * 2 + sixteen % 2
    home = (sixteen % 8) // 2
    down_row = (y2 - home) % 4
    up_row = (home - y2) % 4
    table = jnp.concatenate(
        [
            source,
            pair_member[1:],
            (residue - long_start) % 16,
            jnp.where(pair_row[1:] == y2, 1, -1),
            jnp.where(down_row == 3, 14, 5 * down_row) + within,
            (y2 - pair_row[:1]) % 2 * 5 + 4,
            4 * up_row + (up_row > 0) + within,
        ]
    )
    members = jnp.arange(8, dtype=i32)[:, None, None]
    is_long = jnp.tile(source, 2)[:, None, None] == members
    is_first = (pair_member[0] == members) & (pair_row[0] == y2)

    halves = received.reshape(2, 4, 128, 1152)[:, :, :, 1024:]
    long_keys = jnp.where((source > 3)[:, None, None], halves[1], halves[0])
    pair_key = lax.dynamic_slice(received, (pair_member[0], 0, 1024), (1, 128, 128))
    long_keys = jnp.concatenate([long_keys, pair_key], axis=0)

    chosen = choose(target, down_weight, up_weight.reshape(residents, 16, 128))
    chosen, long_keys, own_value = lax.optimization_barrier((chosen, long_keys, own_value))
    fetched = exchange(chosen, "grp")
    keys = jnp.concatenate(
        [
            long_keys,
            row_shift(long_keys, 1),
            row_shift(long_keys[:4], 2),
            row_shift(long_keys[:4], 3),
        ],
        axis=0,
    )
    partial = long_attention(table, received, keys)

    picked, _ = lax.optimization_barrier((pick(block_place, fetched), partial))
    weights = exchange(picked, "seq")
    last = row_shift(partial[13:18], 3)
    head_value = (
        partial[:4].astype(F32)
        + row_shift(partial[5:9], 1).astype(F32)
        + row_shift(partial[9:13], 2).astype(F32)
        + last[:4].astype(F32)
    ).astype(BF16)
    first_value = partial[4] + last[4]
    head_value = jnp.where(
        is_long,
        jnp.concatenate([head_value, head_value], axis=0),
        jnp.where(is_first, first_value, partial[18]),
    )
    head_value, weights = lax.optimization_barrier((head_value, weights))
    far = exchange(head_value, "seq", COLUMN)

    parts = exchange(terms(flags, x, weights, far, own_value), "seq")
    sums = exchange(segment_sum(block_place, parts), "grp")
    return adapter_sum(target, sums)


def solution(mesh):
    rows = P(("grp", "seq"), None)
    return jax.shard_map(
        local,
        mesh=mesh,
        in_specs=(rows,) * 4 + (P("grp", None, "seq"), P("grp", "seq", None)) + (P(),) * 3,
        out_specs=(P("grp", None, "seq"), P("grp", "seq", None)),
        check_vma=False,
    )
```

time: 220 us -> 200 us (0.909)
  waiting for transfers between devices: 50.2 us -> 27.9 us
  blocking collectives: 32 us -> 49.9 us
  between operations: 16.9 us -> 6.61 us
  other arithmetic: 11.8 us -> 8.2 us
    all_to_all x3 -> x4, waiting for transfers between devices: 37.4 us -> 11.5 us  [exchange(): lax.all_to_all(value, axis, 0, 0, axis_index_groups=groups, tiled=True)]
    all_to_all x2, blocking collectives: 32 us -> 49.9 us  [exchange(): lax.all_to_all(value, axis, 0, 0, axis_index_groups=groups, tiled=True)]
    all_to_all x3 -> x4, starting transfers between devices: 35.6 us -> 44.8 us  [exchange(): lax.all_to_all(value, axis, 0, 0, axis_index_groups=groups, tiled=True)]
    ppermute x2 -> x0, starting transfers between devices: 5.34 us -> none  [the longest x1 4.06 us: local(): left = lax.ppermute(k, 'seq', [(b, b + 1) for b in range(31)])]
    ppermute x6, waiting for transfers between devices: 12.7 us -> 16.4 us  [row_shift(): return lax.ppermute(value, 'seq', pairs)]
    ppermute x6, starting transfers between devices: 28.9 us -> 26 us  [row_shift(): return lax.ppermute(value, 'seq', pairs)]
    concatenate x4 -> x2, other arithmetic: 2.54 us -> 0.1 us  [the longest x1 0.08 us: local(): jnp.concatenate([long_keys, row_shift(long_keys, 1), row_shift(long_keys[...]
    unnamed x22 -> x10, local copies, waits for them, and re-layouts: 2.36 us -> 0.02 us
  transfers between devices with their start and end apart: 12 -> 10, of which waited for: 6 -> 7; matrix products, arithmetic and copies ran while one was open for 5% -> 6% of each run, Pallas kernels for 12% -> 9%
where the time goes in v2:
time: 200 us; the launch traced here: 199 us
  starting transfers between devices  70.8 us (35%)
  blocking collectives  49.9 us (25%)
  Pallas kernels  31.1 us (16%)
  waiting for transfers between devices  27.9 us (14%)
  other arithmetic  8.2 us (4%)
  between operations  6.61 us (3%)
  local copies, waits for them, and re-layouts  4.71 us (2%)
    all_to_all x2, blocking collectives, exchange(): lax.all_to_all(value, axis, 0, 0, axis_index_groups=groups, tiled=True)  49.9 us
    all_to_all x4, starting transfers between devices, exchange(): lax.all_to_all(value, axis, 0, 0, axis_index_groups=groups, tiled=True)  44.8 us
    ppermute x6, starting transfers between devices, row_shift(): return lax.ppermute(value, 'seq', pairs)  26 us
    ppermute x6, waiting for transfers between devices, row_shift(): return lax.ppermute(value, 'seq', pairs)  16.4 us
    all_to_all x4, waiting for transfers between devices, exchange(): lax.all_to_all(value, axis, 0, 0, axis_index_groups=groups, tiled=True)  11.5 us
    pallas_call x1, Pallas kernels, long_attention(): pl.pallas_call(long_kernel, name='long', out_shape=jax.ShapeDtypeStruct((...  9.48 us
    pallas_call x1, Pallas kernels, short_attention(): pl.pallas_call(short_kernel, name='short', out_shape=jax.ShapeDtypeStruct...  6.91 us
  transfers between devices with their start and end apart: 10, of which 7 were waited for; matrix products, arithmetic and copies ran while one was open for 6% of the time, Pallas kernels for 9%

profile of v2, /device:TPU:1, one launch (start us, length us, event | category | flops | bytes accessed | tf_op | source)
XLA Modules:
  0.0 199.2 jit_solution(16789116617934108341)
XLA Ops:
  0.6 3.9 %pack.1 = bf16[8,128,1152]{2,1,0:T(8,128)(2,1)} custom-call(bf16[128,4096]{1,0:T(8,128)(2,1)} %q_ref.3, bf16[128,4096]{1,0:T(8,128)(2,1)} %g_ref.3, bf16[128,1024]{1,0:T(8,128)(2,1)} %k_ref.3), custom_call_target="tpu_custom_call" | custom-call | bytes 5242880 | tf_op jit(solution)/shard_map/pack/pallas_call | solution.py:53
  4.5 6.0 %all-to-all-start = ((bf16[8,128,1152]{2,1,0:T(8,128)(2,1)}), bf16[8,128,1152]{2,1,0:T(8,128)(2,1)S(1)}, u32[]{:S(2)}, u32[]{:S(2)}) async-start(bf16[8,128,1152]{2,1,0:T(8,128)(2,1)} %pack.1), calls=%async_computation | async-start | bytes 4718592 | tf_op jit(solution)/shard_map/all_to_all | solution.py:314
  21.4 6.9 %short.1.own_ref = bf16[128,1024]{1,0:T(8,128)(2,1)} custom-call(bf16[128,4096]{1,0:T(8,128)(2,1)} %q_ref.3, bf16[128,4096]{1,0:T(8,128)(2,1)} %g_ref.3, bf16[128,1024]{1,0:T(8,128)(2,1)} %k_ref.3), custom_call_target="tpu_custom_call" | custom-call | flops 3221225472 | bytes 4194304 | tf_op jit(solution)/shard_map/short/pallas_call | solution.py:214
  28.4 7.5 %all-to-all-done.own_ref = bf16[8,128,1152]{2,1,0:T(8,128)(2,1)S(1)} async-done(((bf16[8,128,1152]{2,1,0:T(8,128)(2,1)}), bf16[8,128,1152]{2,1,0:T(8,128)(2,1)S(1)}, u32[]{:S(2)}, u32[]{:S(2)}) %all-to-all-start) | async-done | bytes 2359328 | tf_op jit(solution)/shard_map/all_to_all | solution.py:314
  36.0 15.8 %all-to-all-start.1 = ((bf16[32,80,128]{2,1,0:T(8,128)(2,1)}), bf16[32,80,128]{2,1,0:T(8,128)(2,1)}, u32[]{:S(2)}, u32[]{:S(2)}) async-start(bf16[32,80,128]{2,1,0:T(8,128)(2,1)} %choose.1), calls=%async_computation.1 | async-start | bytes 1310720 | tf_op jit(solution)/shard_map/all_to_all | solution.py:314
  53.1 5.0 %collective-permute-start.2 = (bf16[4,128,128]{2,1,0:T(8,128)(2,1)S(1)}, bf16[4,128,128]{2,1,0:T(8,128)(2,1)S(1)}, u32[]{:S(2)}, u32[]{:S(2)}) collective-permute-start(bf16[4,128,128]{2,1,0:T(8,128)(2,1)S(1)} %slice.57), channel_id=1, source_target_pairs={{0,96},{16,112},{32,0},{48,16},{64,32},{80,48},{96,64},{112,80},{1... | collective-permute-start | bytes 393224 | tf_op jit(solution)/shard_map/ppermute | solution.py:324
  58.1 4.4 %collective-permute-start.1 = (bf16[4,128,128]{2,1,0:T(8,128)(2,1)S(1)}, bf16[4,128,128]{2,1,0:T(8,128)(2,1)S(1)}, u32[]{:S(2)}, u32[]{:S(2)}) collective-permute-start(bf16[4,128,128]{2,1,0:T(8,128)(2,1)S(1)} %slice.57), channel_id=1, source_target_pairs={{0,64},{16,80},{32,96},{48,112},{64,0},{80,16},{96,32},{112,48},{1... | collective-permute-start | bytes 393224 | tf_op jit(solution)/shard_map/ppermute | solution.py:324
  62.6 3.3 %collective-permute-start = (bf16[5,128,128]{2,1,0:T(8,128)(2,1)S(1)}, bf16[5,128,128]{2,1,0:T(8,128)(2,1)S(1)}, u32[]{:S(2)}, u32[]{:S(2)}) collective-permute-start(bf16[5,128,128]{2,1,0:T(8,128)(2,1)S(1)} %pad_maximum_fusion.1), channel_id=1, source_target_pairs={{0,32},{16,48},{32,64},{48,80},{64,96},{80,112},{96,0},{112,16},{1... | collective-permute-start | bytes 491528 | tf_op jit(solution)/shard_map/ppermute | solution.py:324
  69.9 1.9 collective-permute-done.1
  73.0 9.5 %long.1 = bf16[19,128,128]{2,1,0:T(8,128)(2,1)S(1)} custom-call(s32[43]{0:T(128)S(1)} %concatenate.16.tab_ref, bf16[8,128,1152]{2,1,0:T(8,128)(2,1)S(1)} %all-to-all-done.own_ref, bf16[18,128,128]{2,1,0:T(8,128)(2,1)S(1)} %pad_maximum_fusion.key_ref), custom_call_target="tpu_custom_call" | custom-call | flops 6442450944 | bytes 4194304 | tf_op jit(solution)/shard_map/long/pallas_call | solution.py:172
  82.5 2.1 %pick.1 = bf16[32,80,128]{2,1,0:T(8,128)(2,1)} custom-call(s32[32]{0:T(128)} %get-tuple-element.19.tab_ref, bf16[32,80,128]{2,1,0:T(8,128)(2,1)} %all-to-all-done.1.in_ref), custom_call_target="tpu_custom_call" | custom-call | bytes 1048576 | tf_op jit(solution)/shard_map/pick/pallas_call | solution.py:88
  84.6 15.0 %all-to-all-start.2 = ((bf16[32,80,128]{2,1,0:T(8,128)(2,1)}), bf16[32,80,128]{2,1,0:T(8,128)(2,1)S(1)}, u32[]{:S(2)}, u32[]{:S(2)}) async-start(bf16[32,80,128]{2,1,0:T(8,128)(2,1)} %pick.1), calls=%async_computation.2 | async-start | bytes 1310720 | tf_op jit(solution)/shard_map/all_to_all | solution.py:314
  100.3 5.2 %collective-permute-start.5 = (bf16[5,128,128]{2,1,0:T(8,128)(2,1)S(1)}, bf16[5,128,128]{2,1,0:T(8,128)(2,1)S(1)}, u32[]{:S(2)}, u32[]{:S(2)}) collective-permute-start(bf16[5,128,128]{2,1,0:T(8,128)(2,1)S(1)} %slice.71), channel_id=1, source_target_pairs={{0,96},{16,112},{32,0},{48,16},{64,32},{80,48},{96,64},{112,80},{1... | collective-permute-start | bytes 491528 | tf_op jit(solution)/shard_map/ppermute | solution.py:324
  105.6 4.0 %collective-permute-start.4 = (bf16[4,128,128]{2,1,0:T(8,128)(2,1)S(1)}, bf16[4,128,128]{2,1,0:T(8,128)(2,1)S(1)}, u32[]{:S(2)}, u32[]{:S(2)}) collective-permute-start(bf16[4,128,128]{2,1,0:T(8,128)(2,1)S(1)} %get-tuple-element.27), channel_id=1, source_target_pairs={{0,64},{16,80},{32,96},{48,112},{64,0},{80,16},{96,32},{112,48},{1... | collective-permute-start | bytes 393224 | tf_op jit(solution)/shard_map/ppermute | solution.py:324
  109.6 4.0 %collective-permute-start.3 = (bf16[4,128,128]{2,1,0:T(8,128)(2,1)S(1)}, bf16[4,128,128]{2,1,0:T(8,128)(2,1)S(1)}, u32[]{:S(2)}, u32[]{:S(2)}) collective-permute-start(bf16[4,128,128]{2,1,0:T(8,128)(2,1)S(1)} %get-tuple-element.26), channel_id=1, source_target_pairs={{0,32},{16,48},{32,64},{48,80},{64,96},{80,112},{96,0},{112,16},{1... | collective-permute-start | bytes 393224 | tf_op jit(solution)/shard_map/ppermute | solution.py:324
  113.6 10.2 %collective-permute-done.5 = bf16[5,128,128]{2,1,0:T(8,128)(2,1)S(1)} collective-permute-done((bf16[5,128,128]{2,1,0:T(8,128)(2,1)S(1)}, bf16[5,128,128]{2,1,0:T(8,128)(2,1)S(1)}, u32[]{:S(2)}, u32[]{:S(2)}) %collective-permute-start.5) | collective-permute-done | bytes 163872 | tf_op jit(solution)/shard_map/ppermute | solution.py:324
  123.8 2.1 %collective-permute-done.4 = bf16[4,128,128]{2,1,0:T(8,128)(2,1)S(1)} collective-permute-done((bf16[4,128,128]{2,1,0:T(8,128)(2,1)S(1)}, bf16[4,128,128]{2,1,0:T(8,128)(2,1)S(1)}, u32[]{:S(2)}, u32[]{:S(2)}) %collective-permute-start.4) | collective-permute-done | bytes 131104 | tf_op jit(solution)/shard_map/ppermute | solution.py:324
  127.8 8.0 %all-to-all-start.3 = ((bf16[8,128,128]{2,1,0:T(8,128)(2,1)}), bf16[8,128,128]{2,1,0:T(8,128)(2,1)S(1)}, u32[]{:S(2)}, u32[]{:S(2)}) async-start(bf16[8,128,128]{2,1,0:T(8,128)(2,1)} %maximum_select_fusion), calls=%async_computation.3 | async-start | bytes 524288 | tf_op jit(solution)/shard_map/all_to_all | solution.py:314
  138.4 4.0 %all-to-all-done.3.far_ref = bf16[8,128,128]{2,1,0:T(8,128)(2,1)S(1)} async-done(((bf16[8,128,128]{2,1,0:T(8,128)(2,1)}), bf16[8,128,128]{2,1,0:T(8,128)(2,1)S(1)}, u32[]{:S(2)}, u32[]{:S(2)}) %all-to-all-start.3) | async-done | bytes 262176 | tf_op jit(solution)/shard_map/all_to_all | solution.py:314
  142.4 2.2 %terms.1 = bf16[32,80,128]{2,1,0:T(8,128)(2,1)S(1)} custom-call(s32[2]{0:T(128)S(1)} %add_convert_fusion.1.tab_ref, bf16[128,4096]{1,0:T(8,128)(2,1)S(1)} %copy-done, bf16[32,80,128]{2,1,0:T(8,128)(2,1)S(1)} %all-to-all-done.2.w_ref, bf16[8,128,128]{2,1,0:T(8,128)(2,1)S(1)} %all-to-all-done.3.far_ref, bf16[128,1024]{1,0:T(8,128)(2,1)S(1)} %copy-done.1), custom_call_target="tpu_custom_call" | custom-call | flops 1073741824 | bytes 4194304 | tf_op jit(solution)/shard_map/terms/pallas_call | solution.py:257
  144.6 20.8 %all_to_all.30.in_ref = bf16[32,80,128]{2,1,0:T(8,128)(2,1)} all-to-all(bf16[32,80,128]{2,1,0:T(8,128)(2,1)S(1)} %terms.1), channel_id=1, replica_groups=mesh['seq'=32,'grp'=16] {'seq'}, dimensions={0} | all-to-all | bytes 1310720 | tf_op jit(solution)/shard_map/all_to_all | solution.py:314
  165.4 2.3 %segments.1 = bf16[32,80,128]{2,1,0:T(8,128)(2,1)} custom-call(s32[32]{0:T(128)} %get-tuple-element.19.tab_ref, bf16[32,80,128]{2,1,0:T(8,128)(2,1)} %all_to_all.30.in_ref), custom_call_target="tpu_custom_call" | custom-call | tf_op jit(solution)/shard_map/segments/pallas_call | solution.py:281
  167.7 29.2 %all_to_all.31.in_ref = bf16[32,80,128]{2,1,0:T(8,128)(2,1)} all-to-all(bf16[32,80,128]{2,1,0:T(8,128)(2,1)} %segments.1), channel_id=1, replica_groups=mesh['seq'=32,'grp'=16] {'grp'}, dimensions={0} | all-to-all | bytes 1310720 | tf_op jit(solution)/shard_map/all_to_all | solution.py:314
  196.8 2.3 %adapters.1 = (f32[16,64,128]{2,1,0:T(8,128)}, f32[16,2,1024]{2,1,0:T(2,128)}) custom-call(s32[32]{0:T(128)} %reshape.139.tab_ref, bf16[32,80,128]{2,1,0:T(8,128)(2,1)} %all_to_all.31.in_ref), custom_call_target="tpu_custom_call" | custom-call | tf_op jit(solution)/shard_map/adapters/pallas_call | solution.py:300
  (53 shorter events, 16.8 us)
Async XLA Ops:
  4.5 10.7 %copy-start.3 = (s32[16,16]{1,0:T(8,128)S(1)}, s32[16,16]{1,0:T(8,128)}, u32[]{:S(2)}) copy-start(s32[16,16]{1,0:T(8,128)} %param.15) | copy-start | bytes 3076
  4.5 10.7 %copy-start.4 = (s32[256]{0:T(256)S(1)}, s32[256]{0:T(256)}, u32[]{:S(2)}) copy-start(s32[256]{0:T(256)} %param.17) | copy-start | bytes 3076
  4.5 12.4 %copy-start.2 = (bf16[16,2,1024]{2,1,0:T(2,128)(2,1)S(1)}, bf16[16,2,1024]{2,1,0:T(2,128)(2,1)}, u32[]{:S(2)}) copy-start(bf16[16,2,1024]{2,1,0:T(2,128)(2,1)} %param.14) | copy-start | bytes 196612
  4.5 31.3 %all-to-all-start = ((bf16[8,128,1152]{2,1,0:T(8,128)(2,1)}), bf16[8,128,1152]{2,1,0:T(8,128)(2,1)S(1)}, u32[]{:S(2)}, u32[]{:S(2)}) async-start(bf16[8,128,1152]{2,1,0:T(8,128)(2,1)} %pack.1), calls=%async_computation | async-start | bytes 4718592 | tf_op jit(solution)/shard_map/all_to_all | solution.py:314
  36.0 46.5 %all-to-all-start.1 = ((bf16[32,80,128]{2,1,0:T(8,128)(2,1)}), bf16[32,80,128]{2,1,0:T(8,128)(2,1)}, u32[]{:S(2)}, u32[]{:S(2)}) async-start(bf16[32,80,128]{2,1,0:T(8,128)(2,1)} %choose.1), calls=%async_computation.1 | async-start | bytes 1310720 | tf_op jit(solution)/shard_map/all_to_all | solution.py:314
  53.1 16.8 %collective-permute-start.2 = (bf16[4,128,128]{2,1,0:T(8,128)(2,1)S(1)}, bf16[4,128,128]{2,1,0:T(8,128)(2,1)S(1)}, u32[]{:S(2)}, u32[]{:S(2)}) collective-permute-start(bf16[4,128,128]{2,1,0:T(8,128)(2,1)S(1)} %slice.57), channel_id=1, source_target_pairs={{0,96},{16,112},{32,0},{48,16},{64,32},{80,48},{96,64},{112,80},{1... | collective-permute-start | bytes 393224 | tf_op jit(solution)/shard_map/ppermute | solution.py:324
  58.1 13.7 %collective-permute-start.1 = (bf16[4,128,128]{2,1,0:T(8,128)(2,1)S(1)}, bf16[4,128,128]{2,1,0:T(8,128)(2,1)S(1)}, u32[]{:S(2)}, u32[]{:S(2)}) collective-permute-start(bf16[4,128,128]{2,1,0:T(8,128)(2,1)S(1)} %slice.57), channel_id=1, source_target_pairs={{0,64},{16,80},{32,96},{48,112},{64,0},{80,16},{96,32},{112,48},{1... | collective-permute-start | bytes 393224 | tf_op jit(solution)/shard_map/ppermute | solution.py:324
  62.6 10.3 %collective-permute-start = (bf16[5,128,128]{2,1,0:T(8,128)(2,1)S(1)}, bf16[5,128,128]{2,1,0:T(8,128)(2,1)S(1)}, u32[]{:S(2)}, u32[]{:S(2)}) collective-permute-start(bf16[5,128,128]{2,1,0:T(8,128)(2,1)S(1)} %pad_maximum_fusion.1), channel_id=1, source_target_pairs={{0,32},{16,48},{32,64},{48,80},{64,96},{80,112},{96,0},{112,16},{1... | collective-permute-start | bytes 491528 | tf_op jit(solution)/shard_map/ppermute | solution.py:324
  82.5 59.9 %copy-start = (bf16[128,4096]{1,0:T(8,128)(2,1)S(1)}, bf16[128,4096]{1,0:T(8,128)(2,1)}, u32[]{:S(2)}) copy-start(bf16[128,4096]{1,0:T(8,128)(2,1)} %x_ref.1) | copy-start | bytes 3145732
  82.5 59.9 %copy-start.1 = (bf16[128,1024]{1,0:T(8,128)(2,1)S(1)}, bf16[128,1024]{1,0:T(8,128)(2,1)}, u32[]{:S(2)}) copy-start(bf16[128,1024]{1,0:T(8,128)(2,1)} %short.1.own_ref) | copy-start | bytes 786436
  84.6 43.2 %all-to-all-start.2 = ((bf16[32,80,128]{2,1,0:T(8,128)(2,1)}), bf16[32,80,128]{2,1,0:T(8,128)(2,1)S(1)}, u32[]{:S(2)}, u32[]{:S(2)}) async-start(bf16[32,80,128]{2,1,0:T(8,128)(2,1)} %pick.1), calls=%async_computation.2 | async-start | bytes 1310720 | tf_op jit(solution)/shard_map/all_to_all | solution.py:314
  100.3 23.5 %collective-permute-start.5 = (bf16[5,128,128]{2,1,0:T(8,128)(2,1)S(1)}, bf16[5,128,128]{2,1,0:T(8,128)(2,1)S(1)}, u32[]{:S(2)}, u32[]{:S(2)}) collective-permute-start(bf16[5,128,128]{2,1,0:T(8,128)(2,1)S(1)} %slice.71), channel_id=1, source_target_pairs={{0,96},{16,112},{32,0},{48,16},{64,32},{80,48},{96,64},{112,80},{1... | collective-permute-start | bytes 491528 | tf_op jit(solution)/shard_map/ppermute | solution.py:324
  105.6 20.4 %collective-permute-start.4 = (bf16[4,128,128]{2,1,0:T(8,128)(2,1)S(1)}, bf16[4,128,128]{2,1,0:T(8,128)(2,1)S(1)}, u32[]{:S(2)}, u32[]{:S(2)}) collective-permute-start(bf16[4,128,128]{2,1,0:T(8,128)(2,1)S(1)} %get-tuple-element.27), channel_id=1, source_target_pairs={{0,64},{16,80},{32,96},{48,112},{64,0},{80,16},{96,32},{112,48},{1... | collective-permute-start | bytes 393224 | tf_op jit(solution)/shard_map/ppermute | solution.py:324
  109.6 17.4 %collective-permute-start.3 = (bf16[4,128,128]{2,1,0:T(8,128)(2,1)S(1)}, bf16[4,128,128]{2,1,0:T(8,128)(2,1)S(1)}, u32[]{:S(2)}, u32[]{:S(2)}) collective-permute-start(bf16[4,128,128]{2,1,0:T(8,128)(2,1)S(1)} %get-tuple-element.26), channel_id=1, source_target_pairs={{0,32},{16,48},{32,64},{48,80},{64,96},{80,112},{96,0},{112,16},{1... | collective-permute-start | bytes 393224 | tf_op jit(solution)/shard_map/ppermute | solution.py:324
  127.8 14.5 %all-to-all-start.3 = ((bf16[8,128,128]{2,1,0:T(8,128)(2,1)}), bf16[8,128,128]{2,1,0:T(8,128)(2,1)S(1)}, u32[]{:S(2)}, u32[]{:S(2)}) async-start(bf16[8,128,128]{2,1,0:T(8,128)(2,1)} %maximum_select_fusion), calls=%async_computation.3 | async-start | bytes 524288 | tf_op jit(solution)/shard_map/all_to_all | solution.py:314

commit v3 on v2

--- a/solution.py
+++ b/solution.py
@@ -13,8 +13,9 @@
 CAP = 2
 ROWS = 80
 NEG = -1e30
-FACTOR = 1.0 / math.sqrt(HEAD_DIM)
-
+FACTOR = math.log2(math.e) / math.sqrt(HEAD_DIM)
+
+ROW = [[8 * x + 2 * q + p for q in range(4)] for x in range(4) for p in range(2)]
 COLUMN = [[8 * x + 2 * q + p for x in range(4) for p in range(2)] for q in range(4)]
 
 VMEM = pl.BlockSpec(memory_space=pltpu.VMEM)
@@ -122,7 +123,7 @@
             return pl.ds(pl.multiple_of(base + c * 256, 256), 256)
 
         def scores(c):
-            return dot_nt(keys[rows(c), :], queries) * FACTOR
+            return dot_nt(keys[rows(c), :], queries)
 
         def fold(s):
             return jnp.max(s.reshape(32, 8, 512), axis=0)
@@ -141,7 +142,7 @@
         top = jnp.max(top, axis=0, keepdims=True)
 
         def second(c, total):
-            e = jnp.exp(sc[c] - top)
+            e = jnp.exp2((sc[c] - top) * FACTOR)
             sc[c] = e
             return total + jnp.sum(e.reshape(32, 8, 512), axis=0)
 
@@ -178,7 +179,7 @@
             grid=(5,),
             in_specs=[
                 pl.BlockSpec((1, 128, 1152), lambda i, t: (t[i], 0, 0)),
-                whole(18, 128, 128),
+                whole(20, 128, 128),
             ],
             out_specs=whole(19, 128, 128),
             scratch_shapes=[
@@ -197,9 +198,9 @@
 def short_kernel(q_ref, g_ref, k_ref, out_ref):
     key_at = lax.broadcasted_iota(jnp.int32, (128, 512), 0)
     query_at = lax.broadcasted_iota(jnp.int32, (128, 512), 1) & 127
-    s = dot_nt(k_ref[...], stack_heads(q_ref[...])) * FACTOR
+    s = dot_nt(k_ref[...], stack_heads(q_ref[...]))
     s = jnp.where(key_at <= query_at, s, NEG)
-    e = jnp.exp(s - jnp.max(s, axis=0, keepdims=True))
+    e = jnp.exp2((s - jnp.max(s, axis=0, keepdims=True)) * FACTOR)
     p = (e * (1.0 / jnp.sum(e, axis=0, keepdims=True))).astype(BF16)
     summed = jnp.zeros((128, 128), F32)
     for h in range(4):
@@ -232,11 +233,30 @@
     return (col == (row & 7) * 64 + (row >> 3)).astype(BF16)
 
 
-def terms_kernel(tab_ref, x_ref, w_ref, far_ref, own_ref, out_ref, down):
+def low_kernel(x_ref, w_ref, low_ref, up_ref, down):
     for s in range(32):
         down[:, 128 * s : 128 * (s + 1)] = w_ref[s, :64, :]
-    low = dot_nt(x_ref[...], down[...]).astype(BF16)
-    up = dot_nn(interleave(True), w_ref[:, 64:, :].reshape(512, 128)).astype(BF16)
+    low_ref[...] = dot_nt(x_ref[...], down[...]).astype(BF16)
+    up_ref[...] = dot_nn(interleave(True), w_ref[:, 64:, :].reshape(512, 128)).astype(BF16)
+
+
+def low_rank(x, weights):
+    return pl.pallas_call(
+        low_kernel,
+        name="low",
+        out_shape=(
+            jax.ShapeDtypeStruct((128, 64), BF16),
+            jax.ShapeDtypeStruct((512, 128), BF16),
+        ),
+        in_specs=[VMEM] * 2,
+        out_specs=(VMEM, VMEM),
+        scratch_shapes=[pltpu.VMEM((64, 4096), BF16)],
+        cost_estimate=pl.CostEstimate(flops=1 << 28, bytes_accessed=2 << 20, transcendentals=0),
+    )(x, weights)
+
+
+def terms_kernel(tab_ref, x_ref, low_ref, up_ref, far_ref, own_ref, out_ref):
+    low = low_ref[...]
     near, wide = tab_ref[0] > 0, tab_ref[1] > 0
     back = jnp.zeros((128, 64), F32)
     up_terms = []
@@ -244,26 +264,25 @@
         lanes = slice(c * 128, (c + 1) * 128)
         value = jnp.where(near, own_ref[:, lanes].astype(F32), 0.0)
         value = (value + jnp.where(wide, far_ref[c].astype(F32), 0.0)).astype(BF16)
-        back += dot_nt(value, up[64 * c : 64 * (c + 1), :])
+        back += dot_nt(value, up_ref[64 * c : 64 * (c + 1), :])
         up_terms.append((2.0 * dot_tn(low, value)).astype(BF16))
-    mixed = dot_nn(interleave(False), jnp.concatenate(up_terms, axis=0)).astype(BF16)
-    out_ref[:, 64:, :] = mixed.reshape(32, 16, 128)
     back = (2.0 * back).astype(BF16)
     for s in range(32):
         out_ref[s, :64, :] = dot_tn(back, x_ref[:, 128 * s : 128 * (s + 1)]).astype(BF16)
-
-
-def terms(table, x, weights, far, own):
+    mixed = dot_nn(interleave(False), jnp.concatenate(up_terms, axis=0)).astype(BF16)
+    out_ref[:, 64:, :] = mixed.reshape(32, 16, 128)
+
+
+def terms(table, x, low, up, far, own):
     return pl.pallas_call(
         terms_kernel,
         name="terms",
         out_shape=jax.ShapeDtypeStruct((32, ROWS, 128), BF16),
-        in_specs=[SMEM] + [VMEM] * 4,
+        in_specs=[SMEM] + [VMEM] * 5,
         out_specs=VMEM,
-        scratch_shapes=[pltpu.VMEM((64, 4096), BF16)],
         compiler_params=pltpu.CompilerParams(vmem_limit_bytes=32 << 20),
-        cost_estimate=pl.CostEstimate(flops=1 << 30, bytes_accessed=4 << 20, transcendentals=0),
-    )(table, x, weights, far, own)
+        cost_estimate=pl.CostEstimate(flops=1 << 29, bytes_accessed=4 << 20, transcendentals=0),
+    )(table, x, low, up, far, own)
 
 
 def gather_sum(tab_ref, in_ref, acc):
@@ -368,7 +387,6 @@
     sixteen = (long_start + order) % 16
     within = sixteen // 8 * 2 + sixteen % 2
     home = (sixteen % 8) // 2
-    down_row = (y2 - home) % 4
     up_row = (home - y2) % 4
     table = jnp.concatenate(
         [
@@ -376,8 +394,8 @@
             pair_member[1:],
             (residue - long_start) % 16,
             jnp.where(pair_row[1:] == y2, 1, -1),
-            jnp.where(down_row == 3, 14, 5 * down_row) + within,
-            (y2 - pair_row[:1]) % 2 * 5 + 4,
+            5 * home + within,
+            5 * pair_row[:1] + 4,
             4 * up_row + (up_row > 0) + within,
         ]
     )
@@ -391,21 +409,15 @@
     long_keys = jnp.concatenate([long_keys, pair_key], axis=0)
 
     chosen = choose(target, down_weight, up_weight.reshape(residents, 16, 128))
-    chosen, long_keys, own_value = lax.optimization_barrier((chosen, long_keys, own_value))
+    chosen, long_keys, own_value, table, block_place, flags = lax.optimization_barrier(
+        (chosen, long_keys, own_value, table, block_place, flags)
+    )
     fetched = exchange(chosen, "grp")
-    keys = jnp.concatenate(
-        [
-            long_keys,
-            row_shift(long_keys, 1),
-            row_shift(long_keys[:4], 2),
-            row_shift(long_keys[:4], 3),
-        ],
-        axis=0,
-    )
+    keys = lax.all_gather(long_keys, "seq", axis=0, tiled=True, axis_index_groups=ROW)
+
+    picked, keys = lax.optimization_barrier((pick(block_place, fetched), keys))
+    weights = exchange(picked, "seq")
     partial = long_attention(table, received, keys)
-
-    picked, _ = lax.optimization_barrier((pick(block_place, fetched), partial))
-    weights = exchange(picked, "seq")
     last = row_shift(partial[13:18], 3)
     head_value = (
         partial[:4].astype(F32)
@@ -422,7 +434,7 @@
     head_value, weights = lax.optimization_barrier((head_value, weights))
     far = exchange(head_value, "seq", COLUMN)
 
-    parts = exchange(terms(flags, x, weights, far, own_value), "seq")
+    parts = exchange(terms(flags, x, *low_rank(x, weights), far, own_value), "seq")
     sums = exchange(segment_sum(block_place, parts), "grp")
     return adapter_sum(target, sums)
 

time: 200 us -> 188 us (0.940)
  blocking collectives: 49.9 us -> 73.4 us
  starting transfers between devices: 70.8 us -> 49.4 us
  waiting for transfers between devices: 27.9 us -> 10.2 us
    all_gather x0 -> x1, blocking collectives: none -> 18.8 us  [local(): lax.all_gather(long_keys, 'seq', axis=0, tiled=True, axis_index_groups=ROW)]
    all_to_all x4, starting transfers between devices: 44.8 us -> 32.4 us  [exchange(): lax.all_to_all(value, axis, 0, 0, axis_index_groups=groups, tiled=True)]
    ppermute x6 -> x3, waiting for transfers between devices: 16.4 us -> 6.73 us  [row_shift(): return lax.ppermute(value, 'seq', pairs)]
    ppermute x6 -> x3, starting transfers between devices: 26 us -> 17 us  [row_shift(): return lax.ppermute(value, 'seq', pairs)]
    all_to_all x4, waiting for transfers between devices: 11.5 us -> 3.44 us  [exchange(): lax.all_to_all(value, axis, 0, 0, axis_index_groups=groups, tiled=True)]
    all_to_all x2, blocking collectives: 49.9 us -> 54.5 us  [exchange(): lax.all_to_all(value, axis, 0, 0, axis_index_groups=groups, tiled=True)]
    pallas_call x0 -> x1, Pallas kernels: none -> 2.63 us  [low_rank(): pl.pallas_call(low_kernel, name='low', out_shape=(jax.ShapeDtypeStruct((1...]
  transfers between devices with their start and end apart: 10 -> 7, of which waited for: 7 -> 3; matrix products, arithmetic and copies ran while one was open for 6% -> 7% of each run, Pallas kernels for 9% -> 11%
where the time goes in v3:
time: 188 us; the launch traced here: 187 us
  blocking collectives  73.4 us (39%)
  starting transfers between devices  49.4 us (26%)
  Pallas kernels  32.3 us (17%)
  waiting for transfers between devices  10.2 us (5%)
  other arithmetic  8.14 us (4%)
  between operations  6.77 us (4%)
  local copies, waits for them, and re-layouts  6.54 us (3%)
    all_to_all x2, blocking collectives, exchange(): lax.all_to_all(value, axis, 0, 0, axis_index_groups=groups, tiled=True)  54.5 us
    all_to_all x4, starting transfers between devices, exchange(): lax.all_to_all(value, axis, 0, 0, axis_index_groups=groups, tiled=True)  32.4 us
    all_gather x1, blocking collectives, local(): lax.all_gather(long_keys, 'seq', axis=0, tiled=True, axis_index_groups=ROW)  18.8 us
    ppermute x3, starting transfers between devices, row_shift(): return lax.ppermute(value, 'seq', pairs)  17 us
    pallas_call x1, Pallas kernels, long_attention(): pl.pallas_call(long_kernel, name='long', out_shape=jax.ShapeDtypeStruct((...  8.95 us
    pallas_call x1, Pallas kernels, short_attention(): pl.pallas_call(short_kernel, name='short', out_shape=jax.ShapeDtypeStruct...  6.91 us
    ppermute x3, waiting for transfers between devices, row_shift(): return lax.ppermute(value, 'seq', pairs)  6.73 us
    pallas_call x1, Pallas kernels, pack(): pl.pallas_call(pack_kernel, name='pack', out_shape=jax.ShapeDtypeStruct((...  3.9 us
  transfers between devices with their start and end apart: 7, of which 3 were waited for; matrix products, arithmetic and copies ran while one was open for 7% of the time, Pallas kernels for 11%

profile of v3, /device:TPU:1, one launch (start us, length us, event | category | flops | bytes accessed | tf_op | source)
XLA Modules:
  0.0 186.7 jit_solution(6841972312691660796)
XLA Ops:
  0.6 3.9 %pack.1 = bf16[8,128,1152]{2,1,0:T(8,128)(2,1)} custom-call(bf16[128,4096]{1,0:T(8,128)(2,1)} %q_ref.3, bf16[128,4096]{1,0:T(8,128)(2,1)} %g_ref.3, bf16[128,1024]{1,0:T(8,128)(2,1)} %k_ref.3), custom_call_target="tpu_custom_call" | custom-call | bytes 5242880 | tf_op jit(solution)/shard_map/pack/pallas_call | solution.py:54
  4.5 6.0 %all-to-all-start = ((bf16[8,128,1152]{2,1,0:T(8,128)(2,1)}), bf16[8,128,1152]{2,1,0:T(8,128)(2,1)S(1)}, u32[]{:S(2)}, u32[]{:S(2)}) async-start(bf16[8,128,1152]{2,1,0:T(8,128)(2,1)} %pack.1), calls=%async_computation | async-start | bytes 4718592 | tf_op jit(solution)/shard_map/all_to_all | solution.py:333
  11.3 1.3 fusion.12
  24.2 1.9 %choose.1 = bf16[32,80,128]{2,1,0:T(8,128)(2,1)} custom-call(s32[32]{0:T(128)} %reshape.137.tab_ref, bf16[16,64,128]{2,1,0:T(8,128)(2,1)} %down_ref.1, bf16[16,16,128]{2,1,0:T(8,128)(2,1)} %reshape.138.up_ref), custom_call_target="tpu_custom_call" | custom-call | bytes 1048576 | tf_op jit(solution)/shard_map/choose/pallas_call | solution.py:73
  28.9 6.9 %short.1.own_ref = bf16[128,1024]{1,0:T(8,128)(2,1)} custom-call(bf16[128,4096]{1,0:T(8,128)(2,1)} %q_ref.3, bf16[128,4096]{1,0:T(8,128)(2,1)} %g_ref.3, bf16[128,1024]{1,0:T(8,128)(2,1)} %k_ref.3), custom_call_target="tpu_custom_call" | custom-call | flops 3221225472 | bytes 4194304 | tf_op jit(solution)/shard_map/short/pallas_call | solution.py:215
  36.0 15.8 %all-to-all-start.1 = ((bf16[32,80,128]{2,1,0:T(8,128)(2,1)}), bf16[32,80,128]{2,1,0:T(8,128)(2,1)}, u32[]{:S(2)}, u32[]{:S(2)}) async-start(bf16[32,80,128]{2,1,0:T(8,128)(2,1)} %choose.1), calls=%async_computation.1 | async-start | bytes 1310720 | tf_op jit(solution)/shard_map/all_to_all | solution.py:333
  53.2 18.8 %all_gather.3.key_ref = bf16[20,128,128]{2,1,0:T(8,128)(2,1)S(1)} all-gather(bf16[5,128,128]{2,1,0:T(8,128)(2,1)S(1)} %pad_maximum_fusion), channel_id=1, replica_groups={{0,32,64,96},{16,48,80,112},{128,160,192,224},{144,176,208,240},{256,28..., dimensions={0}, use_global_device_ids=true | all-gather | bytes 819200 | tf_op jit(solution)/shard_map/all_gather | solution.py:416
  72.0 2.0 %pick.1 = bf16[32,80,128]{2,1,0:T(8,128)(2,1)} custom-call(s32[32]{0:T(128)} %get-tuple-element.14.tab_ref, bf16[32,80,128]{2,1,0:T(8,128)(2,1)} %all-to-all-done.1.in_ref), custom_call_target="tpu_custom_call" | custom-call | bytes 1048576 | tf_op jit(solution)/shard_map/pick/pallas_call | solution.py:89
  74.0 7.2 %all-to-all-start.2 = ((bf16[32,80,128]{2,1,0:T(8,128)(2,1)}), bf16[32,80,128]{2,1,0:T(8,128)(2,1)}, u32[]{:S(2)}, u32[]{:S(2)}) async-start(bf16[32,80,128]{2,1,0:T(8,128)(2,1)} %pick.1), calls=%async_computation.2 | async-start | bytes 1310720 | tf_op jit(solution)/shard_map/all_to_all | solution.py:333
  81.2 9.0 %long.1 = bf16[19,128,128]{2,1,0:T(8,128)(2,1)S(1)} custom-call(s32[43]{0:T(128)S(1)} %concatenate.13.tab_ref, bf16[8,128,1152]{2,1,0:T(8,128)(2,1)S(1)} %all-to-all-done.own_ref, bf16[20,128,128]{2,1,0:T(8,128)(2,1)S(1)} %all_gather.3.key_ref), custom_call_target="tpu_custom_call" | custom-call | flops 6442450944 | bytes 4194304 | tf_op jit(solution)/shard_map/long/pallas_call | solution.py:173
  90.2 6.9 %collective-permute-start.2 = (bf16[5,128,128]{2,1,0:T(8,128)(2,1)S(1)}, bf16[5,128,128]{2,1,0:T(8,128)(2,1)S(1)}, u32[]{:S(2)}, u32[]{:S(2)}) collective-permute-start(bf16[5,128,128]{2,1,0:T(8,128)(2,1)S(1)} %slice.66), channel_id=1, source_target_pairs={{0,96},{16,112},{32,0},{48,16},{64,32},{80,48},{96,64},{112,80},{1... | collective-permute-start | bytes 491528 | tf_op jit(solution)/shard_map/ppermute | solution.py:343
  97.1 1.9 %collective-permute-start = (bf16[4,128,128]{2,1,0:T(8,128)(2,1)S(1)}, bf16[4,128,128]{2,1,0:T(8,128)(2,1)S(1)}, u32[]{:S(2)}, u32[]{:S(2)}) collective-permute-start(bf16[4,128,128]{2,1,0:T(8,128)(2,1)S(1)} %get-tuple-element.38), channel_id=1, source_target_pairs={{0,32},{16,48},{32,64},{48,80},{64,96},{80,112},{96,0},{112,16},{1... | collective-permute-start | bytes 393224 | tf_op jit(solution)/shard_map/ppermute | solution.py:343
  99.1 8.2 %collective-permute-start.1 = (bf16[4,128,128]{2,1,0:T(8,128)(2,1)S(1)}, bf16[4,128,128]{2,1,0:T(8,128)(2,1)S(1)}, u32[]{:S(2)}, u32[]{:S(2)}) collective-permute-start(bf16[4,128,128]{2,1,0:T(8,128)(2,1)S(1)} %get-tuple-element.39), channel_id=1, source_target_pairs={{0,64},{16,80},{32,96},{48,112},{64,0},{80,16},{96,32},{112,48},{1... | collective-permute-start | bytes 393224 | tf_op jit(solution)/shard_map/ppermute | solution.py:343
  107.3 6.7 %collective-permute-done.1 = bf16[4,128,128]{2,1,0:T(8,128)(2,1)S(1)} collective-permute-done((bf16[4,128,128]{2,1,0:T(8,128)(2,1)S(1)}, bf16[4,128,128]{2,1,0:T(8,128)(2,1)S(1)}, u32[]{:S(2)}, u32[]{:S(2)}) %collective-permute-start.1) | collective-permute-done | bytes 131104 | tf_op jit(solution)/shard_map/ppermute | solution.py:343
  114.1 0.8 maximum_select_fusion
  114.9 3.4 %all-to-all-start.3 = ((bf16[8,128,128]{2,1,0:T(8,128)(2,1)}), bf16[8,128,128]{2,1,0:T(8,128)(2,1)S(1)}, u32[]{:S(2)}, u32[]{:S(2)}) async-start(bf16[8,128,128]{2,1,0:T(8,128)(2,1)} %maximum_select_fusion), calls=%async_computation.3 | async-start | bytes 524288 | tf_op jit(solution)/shard_map/all_to_all | solution.py:333
  118.3 2.6 %low.1 = (bf16[128,64]{1,0:T(8,128)(2,1)}, bf16[512,128]{1,0:T(8,128)(2,1)}) custom-call(bf16[128,4096]{1,0:T(8,128)(2,1)} %x_ref.3, bf16[32,80,128]{2,1,0:T(8,128)(2,1)} %all-to-all-done.2.w_ref), custom_call_target="tpu_custom_call" | custom-call | flops 268435456 | bytes 2097152 | tf_op jit(solution)/shard_map/low/pallas_call | solution.py:244
  121.0 3.4 %all-to-all-done.3.far_ref = bf16[8,128,128]{2,1,0:T(8,128)(2,1)S(1)} async-done(((bf16[8,128,128]{2,1,0:T(8,128)(2,1)}), bf16[8,128,128]{2,1,0:T(8,128)(2,1)S(1)}, u32[]{:S(2)}, u32[]{:S(2)}) %all-to-all-start.3) | async-done | bytes 262176 | tf_op jit(solution)/shard_map/all_to_all | solution.py:333
  124.4 0.9 copy-done.2
  126.1 1.4 terms.1
  127.5 22.5 %all_to_all.30.in_ref = bf16[32,80,128]{2,1,0:T(8,128)(2,1)} all-to-all(bf16[32,80,128]{2,1,0:T(8,128)(2,1)S(1)} %terms.1), channel_id=1, replica_groups=mesh['seq'=32,'grp'=16] {'seq'}, dimensions={0} | all-to-all | bytes 1310720 | tf_op jit(solution)/shard_map/all_to_all | solution.py:333
  150.1 2.3 %segments.1 = bf16[32,80,128]{2,1,0:T(8,128)(2,1)} custom-call(s32[32]{0:T(128)} %get-tuple-element.14.tab_ref, bf16[32,80,128]{2,1,0:T(8,128)(2,1)} %all_to_all.30.in_ref), custom_call_target="tpu_custom_call" | custom-call | tf_op jit(solution)/shard_map/segments/pallas_call | solution.py:300
  152.4 32.0 %all_to_all.31.in_ref = bf16[32,80,128]{2,1,0:T(8,128)(2,1)} all-to-all(bf16[32,80,128]{2,1,0:T(8,128)(2,1)} %segments.1), channel_id=1, replica_groups=mesh['seq'=32,'grp'=16] {'grp'}, dimensions={0} | all-to-all | bytes 1310720 | tf_op jit(solution)/shard_map/all_to_all | solution.py:333
  184.4 2.3 %adapters.1 = (f32[16,64,128]{2,1,0:T(8,128)}, f32[16,2,1024]{2,1,0:T(2,128)}) custom-call(s32[32]{0:T(128)} %reshape.137.tab_ref, bf16[32,80,128]{2,1,0:T(8,128)(2,1)} %all_to_all.31.in_ref), custom_call_target="tpu_custom_call" | custom-call | tf_op jit(solution)/shard_map/adapters/pallas_call | solution.py:319
  (51 shorter events, 11.7 us)
Async XLA Ops:
  4.5 11.4 %copy-start.5 = (s32[16,16]{1,0:T(8,128)S(1)}, s32[16,16]{1,0:T(8,128)}, u32[]{:S(2)}) copy-start(s32[16,16]{1,0:T(8,128)} %param.15) | copy-start | bytes 3076
  4.5 11.4 %copy-start.6 = (s32[256]{0:T(256)S(1)}, s32[256]{0:T(256)}, u32[]{:S(2)}) copy-start(s32[256]{0:T(256)} %param.17) | copy-start | bytes 3076
  4.5 16.4 %copy-start.4 = (bf16[16,2,1024]{2,1,0:T(2,128)(2,1)S(1)}, bf16[16,2,1024]{2,1,0:T(2,128)(2,1)}, u32[]{:S(2)}) copy-start(bf16[16,2,1024]{2,1,0:T(2,128)(2,1)} %param.14) | copy-start | bytes 196612
  4.5 31.3 %all-to-all-start = ((bf16[8,128,1152]{2,1,0:T(8,128)(2,1)}), bf16[8,128,1152]{2,1,0:T(8,128)(2,1)S(1)}, u32[]{:S(2)}, u32[]{:S(2)}) async-start(bf16[8,128,1152]{2,1,0:T(8,128)(2,1)} %pack.1), calls=%async_computation | async-start | bytes 4718592 | tf_op jit(solution)/shard_map/all_to_all | solution.py:333
  36.0 36.0 %all-to-all-start.1 = ((bf16[32,80,128]{2,1,0:T(8,128)(2,1)}), bf16[32,80,128]{2,1,0:T(8,128)(2,1)}, u32[]{:S(2)}, u32[]{:S(2)}) async-start(bf16[32,80,128]{2,1,0:T(8,128)(2,1)} %choose.1), calls=%async_computation.1 | async-start | bytes 1310720 | tf_op jit(solution)/shard_map/all_to_all | solution.py:333
  74.0 40.9 %all-to-all-start.2 = ((bf16[32,80,128]{2,1,0:T(8,128)(2,1)}), bf16[32,80,128]{2,1,0:T(8,128)(2,1)}, u32[]{:S(2)}, u32[]{:S(2)}) async-start(bf16[32,80,128]{2,1,0:T(8,128)(2,1)} %pick.1), calls=%async_computation.2 | async-start | bytes 1310720 | tf_op jit(solution)/shard_map/all_to_all | solution.py:333
  90.2 34.2 %copy-start = (bf16[128,4096]{1,0:T(8,128)(2,1)S(1)}, bf16[128,4096]{1,0:T(8,128)(2,1)}, u32[]{:S(2)}) copy-start(bf16[128,4096]{1,0:T(8,128)(2,1)} %x_ref.3) | copy-start | bytes 3145732
  90.2 34.2 %copy-start.1 = (bf16[128,1024]{1,0:T(8,128)(2,1)S(1)}, bf16[128,1024]{1,0:T(8,128)(2,1)}, u32[]{:S(2)}) copy-start(bf16[128,1024]{1,0:T(8,128)(2,1)} %short.1.own_ref) | copy-start | bytes 786436
  90.2 17.1 %collective-permute-start.2 = (bf16[5,128,128]{2,1,0:T(8,128)(2,1)S(1)}, bf16[5,128,128]{2,1,0:T(8,128)(2,1)S(1)}, u32[]{:S(2)}, u32[]{:S(2)}) collective-permute-start(bf16[5,128,128]{2,1,0:T(8,128)(2,1)S(1)} %slice.66), channel_id=1, source_target_pairs={{0,96},{16,112},{32,0},{48,16},{64,32},{80,48},{96,64},{112,80},{1... | collective-permute-start | bytes 491528 | tf_op jit(solution)/shard_map/ppermute | solution.py:343
  97.1 10.2 %collective-permute-start = (bf16[4,128,128]{2,1,0:T(8,128)(2,1)S(1)}, bf16[4,128,128]{2,1,0:T(8,128)(2,1)S(1)}, u32[]{:S(2)}, u32[]{:S(2)}) collective-permute-start(bf16[4,128,128]{2,1,0:T(8,128)(2,1)S(1)} %get-tuple-element.38), channel_id=1, source_target_pairs={{0,32},{16,48},{32,64},{48,80},{64,96},{80,112},{96,0},{112,16},{1... | collective-permute-start | bytes 393224 | tf_op jit(solution)/shard_map/ppermute | solution.py:343
  99.1 14.9 %collective-permute-start.1 = (bf16[4,128,128]{2,1,0:T(8,128)(2,1)S(1)}, bf16[4,128,128]{2,1,0:T(8,128)(2,1)S(1)}, u32[]{:S(2)}, u32[]{:S(2)}) collective-permute-start(bf16[4,128,128]{2,1,0:T(8,128)(2,1)S(1)} %get-tuple-element.39), channel_id=1, source_target_pairs={{0,64},{16,80},{32,96},{48,112},{64,0},{80,16},{96,32},{112,48},{1... | collective-permute-start | bytes 393224 | tf_op jit(solution)/shard_map/ppermute | solution.py:343
  114.9 9.5 %all-to-all-start.3 = ((bf16[8,128,128]{2,1,0:T(8,128)(2,1)}), bf16[8,128,128]{2,1,0:T(8,128)(2,1)S(1)}, u32[]{:S(2)}, u32[]{:S(2)}) async-start(bf16[8,128,128]{2,1,0:T(8,128)(2,1)} %maximum_select_fusion), calls=%async_computation.3 | async-start | bytes 524288 | tf_op jit(solution)/shard_map/all_to_all | solution.py:333
  124.4 0.9 copy-start.2
  125.3 0.8 copy-start.3

commit v4 on v3

--- a/solution.py
+++ b/solution.py
@@ -297,13 +297,18 @@
 
 
 def segment_sum(table, parts):
+    rows = pl.BlockSpec((32, 16, 128), lambda i, t: (0, i, 0))
     return pl.pallas_call(
         segment_kernel,
         name="segments",
         out_shape=jax.ShapeDtypeStruct((32, ROWS, 128), BF16),
-        in_specs=[SMEM, VMEM],
-        out_specs=VMEM,
-        scratch_shapes=[pltpu.VMEM((32, ROWS, 128), F32)],
+        grid_spec=pltpu.PrefetchScalarGridSpec(
+            num_scalar_prefetch=1,
+            grid=(ROWS // 16,),
+            in_specs=[rows],
+            out_specs=rows,
+            scratch_shapes=[pltpu.VMEM((32, 16, 128), F32)],
+        ),
     )(table, parts)
 
 

time: 188 us -> 192 us (1.021)
  Pallas kernels: 32.3 us -> 39.5 us
  starting transfers between devices: 49.4 us -> 45.7 us
  blocking collectives: 73.4 us -> 71.2 us
    ppermute x3, starting transfers between devices: 17 us -> 9.64 us  [row_shift(): return lax.ppermute(value, 'seq', pairs)]
    pallas_call x1, Pallas kernels: 8.95 us -> 13.7 us  [long_attention(): pl.pallas_call(long_kernel, name='long', out_shape=jax.ShapeDtypeStruct((...]
    all_to_all x4, starting transfers between devices: 32.4 us -> 36.1 us  [exchange(): lax.all_to_all(value, axis, 0, 0, axis_index_groups=groups, tiled=True)]
    pallas_call x1, Pallas kernels: 2.3 us -> 4.77 us  [segment_sum(): pl.pallas_call(segment_kernel, name='segments', out_shape=jax.ShapeDtypeS...]
    all_to_all x2, blocking collectives: 54.5 us -> 52.4 us  [exchange(): lax.all_to_all(value, axis, 0, 0, axis_index_groups=groups, tiled=True)]
  transfers between devices with their start and end apart: 7 -> 7, of which waited for: 3 -> 4; matrix products, arithmetic and copies ran while one was open for 7% -> 7% of each run, Pallas kernels for 11% -> 13%
where the time goes in v4:
time: 192 us; the launch traced here: 190 us
  blocking collectives  71.2 us (37%)
  starting transfers between devices  45.7 us (24%)
  Pallas kernels  39.5 us (21%)
  waiting for transfers between devices  12.1 us (6%)
  other arithmetic  8.13 us (4%)
  between operations  6.75 us (4%)
  local copies, waits for them, and re-layouts  6.54 us (3%)
    all_to_all x2, blocking collectives, exchange(): lax.all_to_all(value, axis, 0, 0, axis_index_groups=groups, tiled=True)  52.4 us
    all_to_all x4, starting transfers between devices, exchange(): lax.all_to_all(value, axis, 0, 0, axis_index_groups=groups, tiled=True)  36.1 us
    all_gather x1, blocking collectives, local(): lax.all_gather(long_keys, 'seq', axis=0, tiled=True, axis_index_groups=ROW)  18.8 us
    pallas_call x1, Pallas kernels, long_attention(): pl.pallas_call(long_kernel, name='long', out_shape=jax.ShapeDtypeStruct((...  13.7 us
    ppermute x3, starting transfers between devices, row_shift(): return lax.ppermute(value, 'seq', pairs)  9.64 us
    ppermute x3, waiting for transfers between devices, row_shift(): return lax.ppermute(value, 'seq', pairs)  8.01 us
    pallas_call x1, Pallas kernels, short_attention(): pl.pallas_call(short_kernel, name='short', out_shape=jax.ShapeDtypeStruct...  6.9 us
    pallas_call x1, Pallas kernels, segment_sum(): pl.pallas_call(segment_kernel, name='segments', out_shape=jax.ShapeDtypeS...  4.77 us
  transfers between devices with their start and end apart: 7, of which 4 were waited for; matrix products, arithmetic and copies ran while one was open for 7% of the time, Pallas kernels for 13%

profile of v4, /device:TPU:1, one launch (start us, length us, event | category | flops | bytes accessed | tf_op | source)
XLA Modules:
  0.0 190.0 jit_solution(17961762672723513266)
XLA Ops:
  0.6 3.9 %pack.1 = bf16[8,128,1152]{2,1,0:T(8,128)(2,1)} custom-call(bf16[128,4096]{1,0:T(8,128)(2,1)} %q_ref.3, bf16[128,4096]{1,0:T(8,128)(2,1)} %g_ref.3, bf16[128,1024]{1,0:T(8,128)(2,1)} %k_ref.3), custom_call_target="tpu_custom_call" | custom-call | bytes 5242880 | tf_op jit(solution)/shard_map/pack/pallas_call | solution.py:54
  4.5 6.0 %all-to-all-start = ((bf16[8,128,1152]{2,1,0:T(8,128)(2,1)}), bf16[8,128,1152]{2,1,0:T(8,128)(2,1)S(1)}, u32[]{:S(2)}, u32[]{:S(2)}) async-start(bf16[8,128,1152]{2,1,0:T(8,128)(2,1)} %pack.1), calls=%async_computation | async-start | bytes 4718592 | tf_op jit(solution)/shard_map/all_to_all | solution.py:338
  11.3 1.3 fusion.12
  24.2 1.9 choose.1
  28.9 6.9 %short.1.own_ref = bf16[128,1024]{1,0:T(8,128)(2,1)} custom-call(bf16[128,4096]{1,0:T(8,128)(2,1)} %q_ref.3, bf16[128,4096]{1,0:T(8,128)(2,1)} %g_ref.3, bf16[128,1024]{1,0:T(8,128)(2,1)} %k_ref.3), custom_call_target="tpu_custom_call" | custom-call | flops 3221225472 | bytes 4194304 | tf_op jit(solution)/shard_map/short/pallas_call | solution.py:215
  36.0 15.8 %all-to-all-start.1 = ((bf16[32,80,128]{2,1,0:T(8,128)(2,1)}), bf16[32,80,128]{2,1,0:T(8,128)(2,1)}, u32[]{:S(2)}, u32[]{:S(2)}) async-start(bf16[32,80,128]{2,1,0:T(8,128)(2,1)} %choose.1), calls=%async_computation.1 | async-start | bytes 1310720 | tf_op jit(solution)/shard_map/all_to_all | solution.py:338
  53.2 18.8 %all_gather.3.key_ref = bf16[20,128,128]{2,1,0:T(8,128)(2,1)S(1)} all-gather(bf16[5,128,128]{2,1,0:T(8,128)(2,1)S(1)} %pad_maximum_fusion), channel_id=1, replica_groups={{0,32,64,96},{16,48,80,112},{128,160,192,224},{144,176,208,240},{256,28..., dimensions={0}, use_global_device_ids=true | all-gather | bytes 819200 | tf_op jit(solution)/shard_map/all_gather | solution.py:421
  72.0 2.0 %pick.1 = bf16[32,80,128]{2,1,0:T(8,128)(2,1)} custom-call(s32[32]{0:T(128)} %get-tuple-element.14.tab_ref, bf16[32,80,128]{2,1,0:T(8,128)(2,1)} %all-to-all-done.1.in_ref), custom_call_target="tpu_custom_call" | custom-call | bytes 1048576 | tf_op jit(solution)/shard_map/pick/pallas_call | solution.py:89
  74.0 7.2 %all-to-all-start.2 = ((bf16[32,80,128]{2,1,0:T(8,128)(2,1)}), bf16[32,80,128]{2,1,0:T(8,128)(2,1)}, u32[]{:S(2)}, u32[]{:S(2)}) async-start(bf16[32,80,128]{2,1,0:T(8,128)(2,1)} %pick.1), calls=%async_computation.2 | async-start | bytes 1310720 | tf_op jit(solution)/shard_map/all_to_all | solution.py:338
  81.2 13.7 %long.1 = bf16[19,128,128]{2,1,0:T(8,128)(2,1)S(1)} custom-call(s32[43]{0:T(128)S(1)} %concatenate.13.tab_ref, bf16[8,128,1152]{2,1,0:T(8,128)(2,1)S(1)} %all-to-all-done.own_ref, bf16[20,128,128]{2,1,0:T(8,128)(2,1)S(1)} %all_gather.3.key_ref), custom_call_target="tpu_custom_call" | custom-call | flops 6442450944 | bytes 4194304 | tf_op jit(solution)/shard_map/long/pallas_call | solution.py:173
  94.9 3.7 %collective-permute-start.2 = (bf16[5,128,128]{2,1,0:T(8,128)(2,1)S(1)}, bf16[5,128,128]{2,1,0:T(8,128)(2,1)S(1)}, u32[]{:S(2)}, u32[]{:S(2)}) collective-permute-start(bf16[5,128,128]{2,1,0:T(8,128)(2,1)S(1)} %slice.66), channel_id=1, source_target_pairs={{0,96},{16,112},{32,0},{48,16},{64,32},{80,48},{96,64},{112,80},{1... | collective-permute-start | bytes 491528 | tf_op jit(solution)/shard_map/ppermute | solution.py:348
  98.7 2.6 %collective-permute-start = (bf16[4,128,128]{2,1,0:T(8,128)(2,1)S(1)}, bf16[4,128,128]{2,1,0:T(8,128)(2,1)S(1)}, u32[]{:S(2)}, u32[]{:S(2)}) collective-permute-start(bf16[4,128,128]{2,1,0:T(8,128)(2,1)S(1)} %get-tuple-element.38), channel_id=1, source_target_pairs={{0,32},{16,48},{32,64},{48,80},{64,96},{80,112},{96,0},{112,16},{1... | collective-permute-start | bytes 393224 | tf_op jit(solution)/shard_map/ppermute | solution.py:348
  101.3 3.3 %collective-permute-start.1 = (bf16[4,128,128]{2,1,0:T(8,128)(2,1)S(1)}, bf16[4,128,128]{2,1,0:T(8,128)(2,1)S(1)}, u32[]{:S(2)}, u32[]{:S(2)}) collective-permute-start(bf16[4,128,128]{2,1,0:T(8,128)(2,1)S(1)} %get-tuple-element.39), channel_id=1, source_target_pairs={{0,64},{16,80},{32,96},{48,112},{64,0},{80,16},{96,32},{112,48},{1... | collective-permute-start | bytes 393224 | tf_op jit(solution)/shard_map/ppermute | solution.py:348
  104.6 1.6 collective-permute-done.2
  106.3 3.6 %collective-permute-done = bf16[4,128,128]{2,1,0:T(8,128)(2,1)S(1)} collective-permute-done((bf16[4,128,128]{2,1,0:T(8,128)(2,1)S(1)}, bf16[4,128,128]{2,1,0:T(8,128)(2,1)S(1)}, u32[]{:S(2)}, u32[]{:S(2)}) %collective-permute-start) | collective-permute-done | bytes 131104 | tf_op jit(solution)/shard_map/ppermute | solution.py:348
  109.9 2.8 %collective-permute-done.1 = bf16[4,128,128]{2,1,0:T(8,128)(2,1)S(1)} collective-permute-done((bf16[4,128,128]{2,1,0:T(8,128)(2,1)S(1)}, bf16[4,128,128]{2,1,0:T(8,128)(2,1)S(1)}, u32[]{:S(2)}, u32[]{:S(2)}) %collective-permute-start.1) | collective-permute-done | bytes 131104 | tf_op jit(solution)/shard_map/ppermute | solution.py:348
  113.6 7.1 %all-to-all-start.3 = ((bf16[8,128,128]{2,1,0:T(8,128)(2,1)}), bf16[8,128,128]{2,1,0:T(8,128)(2,1)S(1)}, u32[]{:S(2)}, u32[]{:S(2)}) async-start(bf16[8,128,128]{2,1,0:T(8,128)(2,1)} %maximum_select_fusion), calls=%async_computation.3 | async-start | bytes 524288 | tf_op jit(solution)/shard_map/all_to_all | solution.py:338
  120.7 2.6 %low.1 = (bf16[128,64]{1,0:T(8,128)(2,1)}, bf16[512,128]{1,0:T(8,128)(2,1)}) custom-call(bf16[128,4096]{1,0:T(8,128)(2,1)} %x_ref.3, bf16[32,80,128]{2,1,0:T(8,128)(2,1)} %all-to-all-done.2.w_ref), custom_call_target="tpu_custom_call" | custom-call | flops 268435456 | bytes 2097152 | tf_op jit(solution)/shard_map/low/pallas_call | solution.py:244
  123.3 4.0 %all-to-all-done.3.far_ref = bf16[8,128,128]{2,1,0:T(8,128)(2,1)S(1)} async-done(((bf16[8,128,128]{2,1,0:T(8,128)(2,1)}), bf16[8,128,128]{2,1,0:T(8,128)(2,1)S(1)}, u32[]{:S(2)}, u32[]{:S(2)}) %all-to-all-start.3) | async-done | bytes 262176 | tf_op jit(solution)/shard_map/all_to_all | solution.py:338
  129.0 1.4 terms.1
  130.5 18.2 %all_to_all.30.in_ref = bf16[32,80,128]{2,1,0:T(8,128)(2,1)} all-to-all(bf16[32,80,128]{2,1,0:T(8,128)(2,1)S(1)} %terms.1), channel_id=1, replica_groups=mesh['seq'=32,'grp'=16] {'seq'}, dimensions={0} | all-to-all | bytes 1310720 | tf_op jit(solution)/shard_map/all_to_all | solution.py:338
  148.7 4.8 %segments.1 = bf16[32,80,128]{2,1,0:T(8,128)(2,1)} custom-call(s32[32]{0:T(128)} %get-tuple-element.14.tab_ref, bf16[32,80,128]{2,1,0:T(8,128)(2,1)} %all_to_all.30.in_ref), custom_call_target="tpu_custom_call" | custom-call | tf_op jit(solution)/shard_map/segments/pallas_call | solution.py:301
  153.4 34.2 %all_to_all.31.in_ref = bf16[32,80,128]{2,1,0:T(8,128)(2,1)} all-to-all(bf16[32,80,128]{2,1,0:T(8,128)(2,1)} %segments.1), channel_id=1, replica_groups=mesh['seq'=32,'grp'=16] {'grp'}, dimensions={0} | all-to-all | bytes 1310720 | tf_op jit(solution)/shard_map/all_to_all | solution.py:338
  187.6 2.3 %adapters.1 = (f32[16,64,128]{2,1,0:T(8,128)}, f32[16,2,1024]{2,1,0:T(2,128)}) custom-call(s32[32]{0:T(128)} %reshape.137.tab_ref, bf16[32,80,128]{2,1,0:T(8,128)(2,1)} %all_to_all.31.in_ref), custom_call_target="tpu_custom_call" | custom-call | tf_op jit(solution)/shard_map/adapters/pallas_call | solution.py:324
  (51 shorter events, 13.3 us)
Async XLA Ops:
  4.5 11.4 %copy-start.5 = (s32[16,16]{1,0:T(8,128)S(1)}, s32[16,16]{1,0:T(8,128)}, u32[]{:S(2)}) copy-start(s32[16,16]{1,0:T(8,128)} %param.15) | copy-start | bytes 3076
  4.5 11.4 %copy-start.6 = (s32[256]{0:T(256)S(1)}, s32[256]{0:T(256)}, u32[]{:S(2)}) copy-start(s32[256]{0:T(256)} %param.17) | copy-start | bytes 3076
  4.5 16.4 %copy-start.4 = (bf16[16,2,1024]{2,1,0:T(2,128)(2,1)S(1)}, bf16[16,2,1024]{2,1,0:T(2,128)(2,1)}, u32[]{:S(2)}) copy-start(bf16[16,2,1024]{2,1,0:T(2,128)(2,1)} %param.14) | copy-start | bytes 196612
  4.5 31.3 %all-to-all-start = ((bf16[8,128,1152]{2,1,0:T(8,128)(2,1)}), bf16[8,128,1152]{2,1,0:T(8,128)(2,1)S(1)}, u32[]{:S(2)}, u32[]{:S(2)}) async-start(bf16[8,128,1152]{2,1,0:T(8,128)(2,1)} %pack.1), calls=%async_computation | async-start | bytes 4718592 | tf_op jit(solution)/shard_map/all_to_all | solution.py:338
  36.0 36.0 %all-to-all-start.1 = ((bf16[32,80,128]{2,1,0:T(8,128)(2,1)}), bf16[32,80,128]{2,1,0:T(8,128)(2,1)}, u32[]{:S(2)}, u32[]{:S(2)}) async-start(bf16[32,80,128]{2,1,0:T(8,128)(2,1)} %choose.1), calls=%async_computation.1 | async-start | bytes 1310720 | tf_op jit(solution)/shard_map/all_to_all | solution.py:338
  74.0 39.5 %all-to-all-start.2 = ((bf16[32,80,128]{2,1,0:T(8,128)(2,1)}), bf16[32,80,128]{2,1,0:T(8,128)(2,1)}, u32[]{:S(2)}, u32[]{:S(2)}) async-start(bf16[32,80,128]{2,1,0:T(8,128)(2,1)} %pick.1), calls=%async_computation.2 | async-start | bytes 1310720 | tf_op jit(solution)/shard_map/all_to_all | solution.py:338
  94.9 32.4 %copy-start = (bf16[128,4096]{1,0:T(8,128)(2,1)S(1)}, bf16[128,4096]{1,0:T(8,128)(2,1)}, u32[]{:S(2)}) copy-start(bf16[128,4096]{1,0:T(8,128)(2,1)} %x_ref.3) | copy-start | bytes 3145732
  94.9 32.4 %copy-start.1 = (bf16[128,1024]{1,0:T(8,128)(2,1)S(1)}, bf16[128,1024]{1,0:T(8,128)(2,1)}, u32[]{:S(2)}) copy-start(bf16[128,1024]{1,0:T(8,128)(2,1)} %short.1.own_ref) | copy-start | bytes 786436
  94.9 11.3 %collective-permute-start.2 = (bf16[5,128,128]{2,1,0:T(8,128)(2,1)S(1)}, bf16[5,128,128]{2,1,0:T(8,128)(2,1)S(1)}, u32[]{:S(2)}, u32[]{:S(2)}) collective-permute-start(bf16[5,128,128]{2,1,0:T(8,128)(2,1)S(1)} %slice.66), channel_id=1, source_target_pairs={{0,96},{16,112},{32,0},{48,16},{64,32},{80,48},{96,64},{112,80},{1... | collective-permute-start | bytes 491528 | tf_op jit(solution)/shard_map/ppermute | solution.py:348
  98.7 11.2 %collective-permute-start = (bf16[4,128,128]{2,1,0:T(8,128)(2,1)S(1)}, bf16[4,128,128]{2,1,0:T(8,128)(2,1)S(1)}, u32[]{:S(2)}, u32[]{:S(2)}) collective-permute-start(bf16[4,128,128]{2,1,0:T(8,128)(2,1)S(1)} %get-tuple-element.38), channel_id=1, source_target_pairs={{0,32},{16,48},{32,64},{48,80},{64,96},{80,112},{96,0},{112,16},{1... | collective-permute-start | bytes 393224 | tf_op jit(solution)/shard_map/ppermute | solution.py:348
  101.3 11.4 %collective-permute-start.1 = (bf16[4,128,128]{2,1,0:T(8,128)(2,1)S(1)}, bf16[4,128,128]{2,1,0:T(8,128)(2,1)S(1)}, u32[]{:S(2)}, u32[]{:S(2)}) collective-permute-start(bf16[4,128,128]{2,1,0:T(8,128)(2,1)S(1)} %get-tuple-element.39), channel_id=1, source_target_pairs={{0,64},{16,80},{32,96},{48,112},{64,0},{80,16},{96,32},{112,48},{1... | collective-permute-start | bytes 393224 | tf_op jit(solution)/shard_map/ppermute | solution.py:348
  113.6 13.8 %all-to-all-start.3 = ((bf16[8,128,128]{2,1,0:T(8,128)(2,1)}), bf16[8,128,128]{2,1,0:T(8,128)(2,1)S(1)}, u32[]{:S(2)}, u32[]{:S(2)}) async-start(bf16[8,128,128]{2,1,0:T(8,128)(2,1)} %maximum_select_fusion), calls=%async_computation.3 | async-start | bytes 524288 | tf_op jit(solution)/shard_map/all_to_all | solution.py:338
  127.3 0.9 copy-start.2
  128.3 0.8 copy-start.3
